TPU v7x, 256 devices: a whole 4x4x8 slice. The times are simulated.
256 devices in a mesh: block: 8 (over z), tile: 32 (over x, y, core).
Axes of the slice: x: 4, y: 4, z: 8, core: 2. Of those that a mesh axis runs over, the one named last changes fastest.
Arguments:
- acts: bfloat16 [16, 32, 64, 384], P('block', 'tile'), may hold values from -6 to 6
- gamma: float32 [384], replicated, may hold values from 0.25 to 1.75
- beta: float32 [384], replicated, may hold values from -3 to 3
- weights: bfloat16 [384, 27, 192], P('tile'), may hold values from -0.0625 to 0.0625
- cotangent: bfloat16 [16, 64, 128, 192], P('block', 'tile'), may hold values from -6 to 6
Outputs:
- d_acts: bfloat16 [16, 32, 64, 384], P('block', 'tile')
- d_weights: float32 [384, 27, 192], P('tile')
All inputs are finite; a program needn't handle non-finite values.
Results may differ from a plain program's by a relative error of at most 0.0029.
Values may be sent and summed in bfloat16 or wider, within the bound.
A program may use at most 128 MiB of HBM per device.

v0:
```python
import jax
import jax.numpy as jnp
from jax import lax
from jax.sharding import PartitionSpec as P

GROUPS = 32


norm_eps = 1e-06


def from_behind(value, axis, steps):
    count = lax.axis_size(axis)
    first, last = (max(0, -steps), min(count, count - steps))
    return lax.ppermute(value, axis, [(source, source + steps) for source in range(first, last)])


def padded_2(value, sides, width):
    for axis, dim in sides:
        size, length = (lax.axis_size(axis), value.shape[dim])
        up = [(i, (i + 1) % size) for i in range(size - 1)]
        down = [(j, i) for i, j in up]
        last = lax.slice_in_dim(value, length - width, length, axis=dim)
        first = lax.slice_in_dim(value, 0, width, axis=dim)
        before = lax.ppermute(last, axis, up)
        after = lax.ppermute(first, axis, down)
        value = jnp.concatenate([before, value, after], axis=dim)
    return value


def group_totals(values, frames, per_group):
    return jnp.sum(values, axis=(1, 2)).reshape(frames, GROUPS, per_group).sum(-1)


def shards(acts, gamma, beta, weights, cotangent):
    frames, low_rows, low_cols, channels = acts.shape
    tiles = lax.axis_size("tile")
    per_group = channels // GROUPS
    group_size = low_rows * tiles * low_cols * per_group
    acts_wide = acts.astype(jnp.float32)
    stat_sum = group_totals(acts_wide, frames, per_group)
    stat_sq = group_totals(acts_wide * acts_wide, frames, per_group)
    stat_sum, stat_sq = lax.psum((stat_sum, stat_sq), "tile")
    group_mean = stat_sum / group_size
    inv_std = lax.rsqrt(stat_sq / group_size - group_mean * group_mean + norm_eps)
    mean_chan = jnp.repeat(group_mean, per_group, axis=1)[:, None, None, :]
    inv_chan = jnp.repeat(inv_std, per_group, axis=1)[:, None, None, :]
    normed = (acts_wide - mean_chan) * inv_chan
    shifted = normed * gamma + beta
    gate_value = jax.nn.sigmoid(shifted)
    hidden = (shifted * gate_value).astype(jnp.bfloat16)
    previous = from_behind(hidden, "block", 1)
    joined = jnp.concatenate([previous, hidden], 0)
    padded = padded_2(joined, (("tile", 1),), 1)
    upsampled = jnp.repeat(jnp.repeat(padded, 2, axis=1), 2, axis=2)[:, 1 : 2 * low_rows + 3]
    upsampled = jnp.pad(upsampled, ((0, 0), (0, 0), (1, 1), (0, 0)))
    following = from_behind(cotangent, "block", -1)
    grad_field = jnp.concatenate([cotangent, following], 0)
    grad_field = padded_2(grad_field, (("tile", 1),), 1)
    grad_field = jnp.pad(grad_field, ((0, 0), (0, 0), (1, 1), (0, 0)))
    up_rows = 2 * low_rows
    up_cols = 2 * low_cols
    num_cells = frames * up_rows * up_cols
    tap_list = [(tap // 9, tap // 3 % 3, tap % 3) for tap in range(27)]
    windows = [
        grad_field[
            2 - tap_t : 2 - tap_t + frames,
            2 - tap_h : 2 - tap_h + up_rows,
            2 - tap_w : 2 - tap_w + up_cols,
        ].reshape(num_cells, -1)
        for tap_t, tap_h, tap_w in tap_list
    ]
    columns = jnp.concatenate(windows, 1)
    piece_rows = lax.all_gather(weights, "tile", axis=0, tiled=True)
    flat_rows = piece_rows.reshape(piece_rows.shape[0], -1)
    back_grad = lax.dot_general(
        columns, flat_rows, (((1,), (1,)), ((), ())), preferred_element_type=jnp.float32
    )
    back_grad = back_grad.reshape(frames, low_rows, 2, low_cols, 2, piece_rows.shape[0])
    act_grad = back_grad.sum(axis=(2, 4))
    silu_slope = gate_value * (1.0 + shifted * (1.0 - gate_value))
    norm_grad = act_grad * silu_slope * gamma
    first_sum = group_totals(norm_grad, frames, per_group)
    second_sum = group_totals(norm_grad * normed, frames, per_group)
    first_sum, second_sum = lax.psum((first_sum, second_sum), "tile")
    first_chan = jnp.repeat(first_sum / group_size, per_group, axis=1)[:, None, None, :]
    second_chan = jnp.repeat(second_sum / group_size, per_group, axis=1)[:, None, None, :]
    d_acts = (inv_chan * (norm_grad - first_chan - normed * second_chan)).astype(jnp.bfloat16)
    flat_grads = cotangent.reshape(num_cells, -1)
    term_list = []
    for tap_t, tap_h, tap_w in tap_list:
        window_h = upsampled[
            tap_t : tap_t + frames, tap_h : tap_h + up_rows, tap_w : tap_w + up_cols
        ].reshape(num_cells, channels)
        term_list.append(
            lax.dot_general(
                window_h, flat_grads, (((0,), (0,)), ((), ())), preferred_element_type=jnp.float32
            )
        )
    whole_terms = jnp.stack(term_list, 1)
    whole_terms = lax.psum(whole_terms, "block")
    d_weights = lax.psum_scatter(whole_terms, "tile", scatter_dimension=0, tiled=True)
    return (d_acts, d_weights)


def solution(mesh):
    placed = (
        P("block", "tile", None, None),
        P(),
        P(),
        P("tile", None, None),
        P("block", "tile", None, None),
    )
    return jax.shard_map(
        shards,
        mesh=mesh,
        in_specs=placed,
        out_specs=(P("block", "tile", None, None), P("tile", None, None)),
        check_vma=False,
    )
```

profile of v0, /device:TPU:2, one launch (start us, length us, event | category | flops | bytes accessed | tf_op | source)
XLA Modules:
  0.0 430.7 jit_solution(1480891718286037013)
XLA Ops:
  7.9 1.3 collective-permute-start
  9.2 1.1 copy.87
  11.7 56.1 %all-reduce.3 = (f32[2,32]{1,0:T(2,128)S(1)}, f32[2,32]{1,0:T(2,128)S(1)}) all-reduce(f32[2,32]{1,0:T(2,128)S(1)} %reduce_sum.86, f32[2,32]{1,0:T(2,128)S(1)} %reduce_sum.84), channel_id=1, replica_groups=mesh['block'=8,'tile'=32] {'tile'}, use_global_device_ids=true, to_apply=%region_5.0 | all-reduce | flops 128 | bytes 1024 | tf_op jit(solution)/shard_map/psum | solution.py:43
  68.8 1.9 collective-permute-start.1
  70.8 5.8 %collective-permute-start.2 = (bf16[4,1,128,192]{2,3,1,0:T(8,128)(2,1)S(1)}, bf16[4,1,128,192]{2,3,1,0:T(8,128)(2,1)S(1)}, u32[]{:S(2)}, u32[]{:S(2)}) collective-permute-start(bf16[4,1,128,192]{2,3,1,0:T(8,128)(2,1)S(1)} %get-tuple-element.44), channel_id=1, source_target_pairs={{1,0},{2,1},{3,2},{4,3},{5,4},{6,5},{7,6},{8,7},{9,8},{10,9},{11,1... | collective-permute-start | bytes 589832 | tf_op jit(solution)/shard_map/ppermute | solution.py:26
  77.9 1.8 collective-permute-done.2
  81.9 1.1 copy.78
  83.8 2.5 fusion.110
  86.9 1.1 copy.88
  88.0 1.8 copy.86
  90.8 1.8 copy.85
  92.6 1.7 copy.112
  94.3 1.8 copy.83
  96.1 1.7 copy.110
  97.7 1.8 copy.82
  99.5 1.7 copy.109
  101.2 1.8 copy.80
  103.0 1.7 copy.107
  104.7 1.8 copy.79
  106.5 1.7 copy.106
  108.2 1.8 copy.77
  110.0 1.7 copy.104
  111.7 1.8 copy.76
  113.5 1.7 copy.103
  115.2 1.8 copy.74
  117.0 1.7 copy.101
  118.7 1.8 copy.73
  120.5 1.7 copy.100
  122.1 1.8 copy.71
  123.9 1.7 copy.98
  125.6 1.8 copy.70
  127.4 1.7 copy.97
  129.1 1.8 copy.68
  130.9 1.7 copy.95
  132.5 1.8 copy.67
  134.3 1.7 copy.94
  136.0 1.8 copy.65
  137.8 1.7 copy.92
  139.5 9.7 %concatenate.111 = bf16[2,1,2,64,2,5184]{5,3,4,2,0,1:T(8,128)(2,1)} concatenate(bf16[2,1,2,64,2,192]{5,3,4,2,0,1:T(8,128)(2,1)} %copy.92, bf16[2,1,2,64,2,192]{5,3,4,2,0,1:T(8,128)(2,1)S(1)} %copy.93, bf16[2,1,2,64,2,192]{5,3,4,2,0,1:T(8,128)(2,1)} %copy.94, bf16[2,1,2,64,2,192]{5,3,4,2,0,1:T(8,128)(2,1)} %copy.95, bf16[2,1,2,64,2,192]{5,3,4,2,0,1:T(8,128)(2,1)S(1)} %copy.96, ...), dimensions={5} | concatenate | bytes 10616832 | tf_op jit(solution)/shard_map/concatenate | solution.py:73
  149.2 8.6 %copy.119 = bf16[384,27,192]{0,2,1:T(8,128)(2,1)} copy(bf16[384,27,192]{2,1,0:T(8,128)(2,1)} %all-gather.2.cloned.1.call-done) | data formatting | bytes 7962624 | tf_op jit(solution)/shard_map/all_gather | solution.py:74
  157.8 6.7 %fusion.8 = f32[2,64,384]{2,1,0:T(8,128)S(1)} fusion(bf16[384,5184,1,1,1]{0,1,4,3,2:T(8,128)(2,1)} %bitcast.286, bf16[2,1,2,64,2,5184]{5,3,4,2,0,1:T(8,128)(2,1)} %concatenate.111), kind=kOutput, calls=%fused_computation.10 | convolution fusion | flops 2038579200 | bytes 9486336 | tf_op jit(solution)/shard_map/dot_general | solution.py:76
  164.7 4.4 %collective-permute-start.3 = (bf16[2,1,64,384]{3,2,1,0:T(8,128)(2,1)S(1)}, bf16[2,1,64,384]{3,2,1,0:T(8,128)(2,1)S(1)}, u32[]{:S(2)}, u32[]{:S(2)}) collective-permute-start(bf16[2,1,64,384]{3,2,1,0:T(8,128)(2,1)S(1)} %get-tuple-element.45), channel_id=1, source_target_pairs={{0,32},{32,64},{64,96},{96,128},{128,160},{160,192},{192,224},{1,3... | collective-permute-start | bytes 294920 | tf_op jit(solution)/shard_map/ppermute | solution.py:15
  169.1 2.2 collective-permute-done.3
  171.3 5.1 %collective-permute-start.5 = (bf16[4,1,64,384]{3,2,1,0:T(8,128)(2,1)S(1)}, bf16[4,1,64,384]{3,2,1,0:T(8,128)(2,1)S(1)}, u32[]{:S(2)}, u32[]{:S(2)}) collective-permute-start(bf16[4,1,64,384]{3,2,1,0:T(8,128)(2,1)S(1)} %pad_maximum_fusion.3), channel_id=1, source_target_pairs={{1,0},{2,1},{3,2},{4,3},{5,4},{6,5},{7,6},{8,7},{9,8},{10,9},{11,1... | collective-permute-start | bytes 589832 | tf_op jit(solution)/shard_map/ppermute | solution.py:26
  176.4 2.1 collective-permute-start.4
  178.5 1.1 collective-permute-done.5
  179.5 5.9 %collective-permute-done.4 = bf16[4,1,64,384]{3,2,1,0:T(8,128)(2,1)S(1)} collective-permute-done((bf16[4,1,64,384]{3,2,1,0:T(8,128)(2,1)S(1)}, bf16[4,1,64,384]{3,2,1,0:T(8,128)(2,1)S(1)}, u32[]{:S(2)}, u32[]{:S(2)}) %collective-permute-start.4) | collective-permute-done | bytes 196640 | tf_op jit(solution)/shard_map/ppermute | solution.py:25
  185.7 3.2 broadcast_in_dim.26
  188.9 5.1 %reshape.166 = bf16[4,6,128,384]{3,2,1,0:T(8,128)(2,1)S(1)} reshape(bf16[4,6,64,2,384]{4,3,2,1,0:T(2,128)(2,1)} %broadcast_in_dim.26) | data formatting | bytes 4718592 | tf_op jit(solution)/shard_map/reshape | solution.py:55
  194.2 1.0 fusion.37
  196.2 1.0 fusion.35
  197.2 1.0 fusion.34
  199.2 1.0 fusion.32
  200.2 1.0 fusion.31
  202.2 1.0 fusion.29
  203.2 1.0 fusion.28
  205.2 1.0 fusion.26
  217.0 1.0 fusion.14
  218.0 1.0 fusion.13
  220.9 12.0 %copy.120 = f32[384,27,192]{2,1,0:T(8,128)} copy(f32[384,27,192]{0,2,1:T(8,128)} %fusion.11) | data formatting | bytes 15925248 | tf_op jit(solution)/shard_map/stack | solution.py:100
  233.4 53.0 %all-reduce.2 = (f32[2,32]{1,0:T(2,128)S(1)}, f32[2,32]{1,0:T(2,128)S(1)}) all-reduce(f32[2,32]{1,0:T(2,128)S(1)} %reduce_sum.92, f32[2,32]{1,0:T(2,128)S(1)} %reduce_sum.90), channel_id=1, replica_groups=mesh['block'=8,'tile'=32] {'tile'}, use_global_device_ids=true, to_apply=%region_12.13 | all-reduce | flops 128 | bytes 1024 | tf_op jit(solution)/shard_map/psum | solution.py:85
  286.4 60.6 %reduce-scatter.2.cloned.1.call-done = f32[12,27,192]{2,1,0:T(8,128)} async-done(((f32[384,27,192]{2,1,0:T(8,128)}), f32[12,27,192]{2,1,0:T(8,128)}) %reduce-scatter.2.cloned.1.call-update) | async-done | bytes 248848 | tf_op jit(solution)/shard_map/reduce_scatter | solution.py:102
  348.1 74.3 %all-reduce.6.cloned.1.call-done = f32[12,27,192]{2,1,0:T(8,128)} async-done(((f32[12,27,192]{2,1,0:T(8,128)}), f32[12,27,192]{2,1,0:T(8,128)}) %all-reduce.6.cloned.1.call-update) | async-done | bytes 248848 | tf_op jit(solution)/shard_map/psum | solution.py:101
  422.4 1.8 copy.177
  (86 shorter events, 27.7 us)
Async XLA Ops:
  7.2 142.0 %all-gather.2.cloned.1.call-start = ((), (), s32[]{:S(2)}) async-start(), calls=%async_computation.1 | async-start | bytes 6488064 | tf_op jit(solution)/shard_map/all_gather | solution.py:74
  7.9 339.1 %reduce-scatter.2.cloned.1.call-start = ((), (), s32[]{:S(2)}) async-start(), calls=%async_computation.2 | async-start | bytes 12976128 | tf_op jit(solution)/shard_map/reduce_scatter | solution.py:102
  7.9 60.8 %collective-permute-start = (bf16[2,2,128,192]{2,3,1,0:T(8,128)(2,1)}, bf16[2,2,128,192]{2,3,1,0:T(8,128)(2,1)S(1)}, u32[]{:S(2)}, u32[]{:S(2)}) collective-permute-start(bf16[2,2,128,192]{2,3,1,0:T(8,128)(2,1)} %param.9), channel_id=1, source_target_pairs={{32,0},{64,32},{96,64},{128,96},{160,128},{192,160},{224,192},{33,... | collective-permute-start | bytes 589832 | tf_op jit(solution)/shard_map/ppermute | solution.py:15
  68.8 9.1 %collective-permute-start.1 = (bf16[4,1,128,192]{2,3,1,0:T(8,128)(2,1)S(1)}, bf16[4,1,128,192]{2,3,1,0:T(8,128)(2,1)S(1)}, u32[]{:S(2)}, u32[]{:S(2)}) collective-permute-start(bf16[4,1,128,192]{2,3,1,0:T(8,128)(2,1)S(1)} %get-tuple-element.43), channel_id=1, source_target_pairs={{0,1},{1,2},{2,3},{3,4},{4,5},{5,6},{6,7},{7,8},{8,9},{9,10},{10,1... | collective-permute-start | bytes 589832 | tf_op jit(solution)/shard_map/ppermute | solution.py:25
  70.8 8.9 %collective-permute-start.2 = (bf16[4,1,128,192]{2,3,1,0:T(8,128)(2,1)S(1)}, bf16[4,1,128,192]{2,3,1,0:T(8,128)(2,1)S(1)}, u32[]{:S(2)}, u32[]{:S(2)}) collective-permute-start(bf16[4,1,128,192]{2,3,1,0:T(8,128)(2,1)S(1)} %get-tuple-element.44), channel_id=1, source_target_pairs={{1,0},{2,1},{3,2},{4,3},{5,4},{6,5},{7,6},{8,7},{9,8},{10,9},{11,1... | collective-permute-start | bytes 589832 | tf_op jit(solution)/shard_map/ppermute | solution.py:26
  157.7 6.7 %copy-start.1 = (bf16[2,1,64,384]{3,2,1,0:T(8,128)(2,1)S(1)}, bf16[2,1,64,384]{3,2,1,0:T(8,128)(2,1)}, u32[]{:S(2)}) copy-start(bf16[2,1,64,384]{3,2,1,0:T(8,128)(2,1)} %param.5) | copy-start | bytes 294916
  157.7 6.7 %copy-start.2 = (f32[384]{0:T(512)S(1)}, f32[384]{0:T(512)}, u32[]{:S(2)}) copy-start(f32[384]{0:T(512)} %param.7) | copy-start | bytes 4612
  157.8 6.7 %copy-start.3 = (f32[384]{0:T(512)S(1)}, f32[384]{0:T(512)}, u32[]{:S(2)}) copy-start(f32[384]{0:T(512)} %param.6) | copy-start | bytes 4612
  164.7 6.6 %collective-permute-start.3 = (bf16[2,1,64,384]{3,2,1,0:T(8,128)(2,1)S(1)}, bf16[2,1,64,384]{3,2,1,0:T(8,128)(2,1)S(1)}, u32[]{:S(2)}, u32[]{:S(2)}) collective-permute-start(bf16[2,1,64,384]{3,2,1,0:T(8,128)(2,1)S(1)} %get-tuple-element.45), channel_id=1, source_target_pairs={{0,32},{32,64},{64,96},{96,128},{128,160},{160,192},{192,224},{1,3... | collective-permute-start | bytes 294920 | tf_op jit(solution)/shard_map/ppermute | solution.py:15
  171.3 8.2 %collective-permute-start.5 = (bf16[4,1,64,384]{3,2,1,0:T(8,128)(2,1)S(1)}, bf16[4,1,64,384]{3,2,1,0:T(8,128)(2,1)S(1)}, u32[]{:S(2)}, u32[]{:S(2)}) collective-permute-start(bf16[4,1,64,384]{3,2,1,0:T(8,128)(2,1)S(1)} %pad_maximum_fusion.3), channel_id=1, source_target_pairs={{1,0},{2,1},{3,2},{4,3},{5,4},{6,5},{7,6},{8,7},{9,8},{10,9},{11,1... | collective-permute-start | bytes 589832 | tf_op jit(solution)/shard_map/ppermute | solution.py:26
  176.4 9.1 %collective-permute-start.4 = (bf16[4,1,64,384]{3,2,1,0:T(8,128)(2,1)S(1)}, bf16[4,1,64,384]{3,2,1,0:T(8,128)(2,1)S(1)}, u32[]{:S(2)}, u32[]{:S(2)}) collective-permute-start(bf16[4,1,64,384]{3,2,1,0:T(8,128)(2,1)S(1)} %pad_maximum_fusion.3), channel_id=1, source_target_pairs={{0,1},{1,2},{2,3},{3,4},{4,5},{5,6},{6,7},{7,8},{8,9},{9,10},{10,1... | collective-permute-start | bytes 589832 | tf_op jit(solution)/shard_map/ppermute | solution.py:25
  188.9 5.3 %copy-start = (bf16[2,2,128,192]{2,3,1,0:T(8,128)(2,1)S(1)}, bf16[2,2,128,192]{2,3,1,0:T(8,128)(2,1)}, u32[]{:S(2)}) copy-start(bf16[2,2,128,192]{2,3,1,0:T(8,128)(2,1)} %param.9) | copy-start | bytes 589828
  232.9 189.4 %all-reduce.6.cloned.1.call-start = ((), (), s32[]{:S(2)}) async-start(), calls=%async_computation.3 | async-start | bytes 786432 | tf_op jit(solution)/shard_map/psum | solution.py:101
Sparse Core Ops, SparseCore 0:
  10.5 56.0 all-gather.1
  233.1 113.8 reduce-scatter.1
  349.3 72.9 all-reduce.5
where the time goes:
time: 433 us; the launch traced here: 431 us
  waiting for transfers between devices  147 us (34%)
  blocking collectives  109 us (25%)
  local copies, waits for them, and re-layouts  102 us (24%)
  matrix products  33.4 us (8%)
  starting transfers between devices  20.7 us (5%)
  between operations  14.2 us (3%)
    psum x1, waiting for transfers between devices, shards(): whole_terms = lax.psum(whole_terms, 'block')  74.3 us
    reduce_scatter x1, waiting for transfers between devices, shards(): lax.psum_scatter(whole_terms, 'tile', scatter_dimension=0, tiled=True)  60.6 us
    psum x1, blocking collectives, shards(): stat_sum, stat_sq = lax.psum((stat_sum, stat_sq), 'tile')  56.1 us
    psum x1, blocking collectives, shards(): first_sum, second_sum = lax.psum((first_sum, second_sum), 'tile')  53 us
    concatenate x28, local copies, waits for them, and re-layouts, shards(): columns = jnp.concatenate(windows, 1)  34.5 us
    slice x26, local copies, waits for them, and re-layouts, shards(): grad_field[2 - tap_t:2 - tap_t + frames, 2 - tap_h:2 - tap_h + up_rows, 2...  33.3 us
    dot_general x27, matrix products, shards(): lax.dot_general(window_h, flat_grads, (((0,), (0,)), ((), ())), preferred...  26.7 us
    another operation x1, local copies, waits for them, and re-layouts, shards(): whole_terms = jnp.stack(term_list, 1)  12 us
  transfers between devices with their start and end apart: 9, of which 7 were waited for; matrix products, arithmetic and copies ran while one was open for 17% of the time, Pallas kernels for 0%

commit v1 on v0

v1 whole, which is shorter than its diff:
```python
import jax
import jax.numpy as jnp
from jax import lax
from jax.experimental import pallas as pl
from jax.experimental.pallas import tpu as pltpu
from jax.sharding import PartitionSpec as P

GROUPS = 32
NORM_EPS = 1e-06
MESH = pl.DeviceIdType.MESH
BF = jnp.bfloat16
F32 = jnp.float32
HALF = 896
CUT = 512
NCOPY = 96
VMEM = pltpu.VMEM


def rows_iota(shape, dim):
    return lax.broadcasted_iota(jnp.int32, shape, dim)


def div12(v):
    return (v * 5462) >> 16


def kernel(n_norm, acts, cot, w, gamma, beta, dacts, dw,
           actbuf, cotbuf, stat_out, stat_in, ghi, glo,
           wy, wx, dpart, sb, rp1, rp2, ra, rb, sm1, sm2,
           dpart2, sb2, rq1, rq2, ra2, rb2, sn1, sn2,
           fin, finb, zin, zred, zout, dsend, drecv, perm_scr, send_sem, recv_sem):
    z = lax.axis_index("block")
    tile = lax.axis_index("tile")
    core = lax.rem(tile, 2)
    q = lax.div(tile, 2)
    y = lax.rem(q, 4)
    x = lax.div(q, 4)

    def chip(cx, cy):
        return {"tile": (cx * 4 + cy) * 2 + core}

    partner = {"tile": tile + 1 - 2 * core}
    outer = {"tile": lax.rem(tile + 2 * core - 1 + 32, 32)}
    xp, xm = chip(lax.rem(x + 1, 4), y), chip(lax.rem(x + 3, 4), y)
    yp, ym = chip(x, lax.rem(y + 1, 4)), chip(x, lax.rem(y + 3, 4))
    plane = [{"tile": lax.rem(q + d, 16) * 2 + core} for d in range(1, 16)]
    column = [{"block": lax.rem(z + k, 8)} for k in range(1, 8)]
    before = {"block": lax.rem(z + 7, 8)}

    copies = []

    def copy(src, dst, device):
        k = len(copies)
        c = pltpu.make_async_remote_copy(
            src_ref=src, dst_ref=dst, send_sem=send_sem.at[k], recv_sem=recv_sem.at[k],
            device_id=device, device_id_type=MESH)
        copies.append(c)
        c.start()
        return c

    barrier = pltpu.get_barrier_semaphore()
    friends = plane + column + [partner, outer]
    for dev in friends:
        pl.semaphore_signal(barrier, inc=1, device_id=dev, device_id_type=MESH)
    pl.semaphore_wait(barrier, len(friends))

    own = pl.ds(1 + 2 * core, 2)
    c_act = copy(acts, actbuf.at[:, core], partner)
    c_z = copy(cot, cotbuf.at[pl.ds(2, 2), own], before)
    c_pair = copy(cot, cotbuf.at[pl.ds(0, 2), own], partner)
    c_edge = copy(cot.at[:, core], cotbuf.at[pl.ds(0, 2), 5 * (1 - core)], outer)

    places = ((y, yp, ym, x, xp, xm), (x, xp, xm, y, yp, ym))

    def gather_start(buf, p, plus, minus):
        return copy(buf.at[p], buf.at[p], plus), copy(buf.at[p], buf.at[p], minus)

    def gather_forward(buf, p, plus, minus, pair):
        pair[0].wait_recv()
        low = lax.rem(p + 3, 4)
        f1 = copy(buf.at[low, :, :, pl.ds(0, CUT)], buf.at[low, :, :, pl.ds(0, CUT)], plus)
        pair[1].wait_recv()
        high = lax.rem(p + 1, 4)
        f2 = copy(buf.at[high, :, :, pl.ds(CUT, HALF - CUT)],
                  buf.at[high, :, :, pl.ds(CUT, HALF - CUT)], minus)
        return f1, f2

    first = []
    for h in range(2):
        p, plus, minus = places[h][:3]
        wy[h, p] = w[h]
        first.append(gather_start(wy.at[h], p, plus, minus))

    actbuf[:, core] = acts[...]
    cotbuf[0:2, own] = cot[...]
    row = rows_iota((192, 384), 0)
    col = rows_iota((192, 384), 1)
    blk = div12(row)
    pick = col == row + 12 * blk + 12 * core
    pick_bf = jnp.where(pick, 1.0, 0.0).astype(BF)
    gcol = jnp.sum(jnp.where(pick, gamma[...], 0.0), axis=1, keepdims=True)
    bcol = jnp.sum(jnp.where(pick, beta[...], 0.0), axis=1, keepdims=True)
    member = rows_iota((192, 128), 1) == div12(rows_iota((192, 128), 0))
    c_act.wait_recv()
    xt = lax.dot_general(pick_bf, actbuf[...].reshape(256, 384), (((1,), (1,)), ((), ())),
                         preferred_element_type=F32)

    def group_sums(u, v):
        lines = []
        for value in (u, v):
            for t in range(2):
                c = jnp.sum(value[:, 128 * t:128 * t + 128], axis=1, keepdims=True)
                lines.append(jnp.sum(jnp.where(member, c, 0.0), axis=0, keepdims=True))
        return jnp.concatenate(lines + [jnp.zeros((4, 128), F32)], axis=0)

    def spread(line):
        return jnp.sum(jnp.where(member, line, 0.0), axis=1, keepdims=True)

    def stats_start(k, total):
        stat_out[k] = total
        return [copy(stat_out.at[k], stat_in.at[k, d], plane[d]) for d in range(15)]

    def stats_end(k, total, cs):
        for d in range(15):
            cs[d].wait_recv()
            total = total + stat_in[k, d]
        return total

    tot1 = group_sums(xt, xt * xt)
    s1 = stats_start(0, tot1)

    second = [gather_forward(wy.at[h], *places[h][:3], first[h]) for h in range(2)]

    c_edge.wait_recv()
    line = 5 * core
    c_edge_f = copy(cotbuf.at[pl.ds(0, 2), line], cotbuf.at[pl.ds(0, 2), line], partner)
    c_z.wait_recv()
    c_pair2 = copy(cotbuf.at[pl.ds(2, 2), own], cotbuf.at[pl.ds(2, 2), own], partner)
    c_edge2 = copy(cotbuf.at[pl.ds(2, 2), 1 + 3 * core],
                   cotbuf.at[pl.ds(2, 2), 5 * (1 - core)], outer)

    third = []
    for h in range(2):
        for f in second[h]:
            f.wait_recv()
        p2, plus2, minus2 = places[h][3:]
        for a in range(3):
            parts = [wy[h, j, a].astype(F32)[0:12] for j in range(4)]
            wx[h, p2, a] = jnp.concatenate(parts, axis=0).astype(BF)
        third.append(gather_start(wx.at[h], p2, plus2, minus2))

    c_edge2.wait_recv()
    c_edge2_f = copy(cotbuf.at[pl.ds(2, 2), line], cotbuf.at[pl.ds(2, 2), line], partner)

    tot1 = stats_end(0, tot1, s1)
    mean_l = tot1[0:2] / n_norm
    inv_l = lax.rsqrt(tot1[2:4] / n_norm - mean_l * mean_l + NORM_EPS)
    wide = lambda m: jnp.concatenate(
        [jnp.broadcast_to(spread(m[t:t + 1]), (192, 128)) for t in range(2)], axis=1)
    inv = wide(inv_l)
    normed = (xt - wide(mean_l)) * inv
    shifted = normed * gcol + bcol
    gate = jax.nn.sigmoid(shifted)
    hidden = (shifted * gate).astype(BF)
    slope = gate * (1.0 + shifted * (1.0 - gate)) * gcol
    r2 = rows_iota((192, 192), 0)
    c2 = rows_iota((192, 192), 1)
    b2 = div12(r2)
    swap = c2 == r2 + 12 * ((b2 & 3) * 4 + (b2 >> 2) - b2)
    swap_bf = jnp.where(swap, 1.0, 0.0).astype(BF)
    hidden_b = jnp.dot(swap_bf, hidden, preferred_element_type=F32).astype(BF)
    hid = (hidden, hidden_b)

    c_pair.wait_recv()
    c_edge_f.wait_recv()
    c_pair2.wait_recv()
    c_edge2_f.wait_recv()
    left = rows_iota((64, 128), 1) < 64
    zero_row = jnp.zeros((1, 128), F32)

    def up(v):
        return jnp.concatenate([v[1:], zero_row], axis=0)

    def down(v):
        return jnp.concatenate([zero_row, v[:-1]], axis=0)

    def put(rows, lane, v):
        hi = v.astype(BF)
        ghi[rows, pl.ds(lane, 128)] = hi
        glo[rows, pl.ds(lane, 128)] = (v - hi.astype(F32)).astype(BF)

    for f in range(4):
        lines = []
        for h in range(6):
            v = cotbuf[f, h].astype(F32)
            if h == 0:
                v = jnp.where(q > 0, v, 0.0)
            if h == 5:
                v = jnp.where(q < 15, v, 0.0)
            if f >= 2:
                v = jnp.where(z < 7, v, 0.0)
            lines.append(v)
        for r in range(2):
            rows = pl.ds(f * 128 + r * 64, 64)
            tops = []
            for b in range(3):
                s = lines[2 * r + 2 - b] + lines[2 * r + 3 - b]
                even, odd, both = s[:, 0:128], s[:, 128:256], s[:, 256:384]
                other = pltpu.roll(both, 64, 1)
                even_t = jnp.where(left, both, other)
                odd_t = jnp.where(left, other, both)
                put(rows, (3 * b) * 128, odd + up(even))
                put(rows, (3 * b + 1) * 128, even + odd)
                put(rows, (3 * b + 2) * 128, down(odd) + even)
                tops += [odd_t + up(even_t), even_t + odd_t, down(odd_t) + even_t]
            for m in range(4):
                put(rows, 1152 + 128 * m, jnp.where(left, tops[2 * m], tops[2 * m + 1]))
            put(rows, 1664, jnp.where(left, tops[8], 0.0))

    def reduce_start(part, sbuf, p, plus, minus, r1, r2_, a_in, b_in):
        opp, nxt, prv = lax.rem(p + 2, 4), lax.rem(p + 1, 4), lax.rem(p + 3, 4)
        lo, hi = pl.ds(0, CUT), pl.ds(CUT, HALF - CUT)
        sbuf[opp] = part[opp].astype(BF)
        o1 = copy(sbuf.at[opp, :, :, lo], r1, plus)
        o2 = copy(sbuf.at[opp, :, :, hi], r2_, minus)
        sbuf[nxt] = part[nxt].astype(BF)
        n1 = copy(sbuf.at[nxt, :, :, hi], a_in.at[:, :, hi], plus)
        sbuf[prv] = part[prv].astype(BF)
        n2 = copy(sbuf.at[prv, :, :, lo], b_in.at[:, :, lo], minus)
        return o1, o2, n1, n2

    def reduce_mid(part, p, plus, minus, r1, r2_, a_in, b_in, s1_, s2_, cs):
        nxt, prv = lax.rem(p + 1, 4), lax.rem(p + 3, 4)
        lo, hi = pl.ds(0, CUT), pl.ds(CUT, HALF - CUT)
        cs[0].wait_recv()
        s1_[...] = (part[nxt, :, :, lo] + r1[...].astype(F32)).astype(BF)
        m1 = copy(s1_, a_in.at[:, :, lo], plus)
        cs[1].wait_recv()
        s2_[...] = (part[prv, :, :, hi] + r2_[...].astype(F32)).astype(BF)
        m2 = copy(s2_, b_in.at[:, :, hi], minus)
        return m1, m2

    def reduce_end(part, p, a_in, b_in, cs, ms):
        for c in (cs[2], cs[3], ms[0], ms[1]):
            c.wait_recv()
        return part[p] + a_in[...].astype(F32) + b_in[...].astype(F32)

    rs_places = (places[1], places[0])
    started = []
    for h in range(2):
        for a in range(3):
            rows, lanes = pl.ds((2 - a) * 128, 256), pl.ds(h * HALF, HALF)
            d = jnp.dot(hid[h], ghi[rows, lanes], preferred_element_type=F32)
            d = d + jnp.dot(hid[h], glo[rows, lanes], preferred_element_type=F32)
            for j in range(4):
                dpart[h, j, a] = d[48 * j:48 * j + 48]
        p, plus, minus = rs_places[h][:3]
        started.append(reduce_start(dpart.at[h], sb.at[h], p, plus, minus,
                                    rp1.at[h], rp2.at[h], ra.at[h], rb.at[h]))

    fourth = [gather_forward(wx.at[h], *places[h][3:], third[h]) for h in range(2)]

    mids = []
    for h in range(2):
        p, plus, minus = rs_places[h][:3]
        mids.append(reduce_mid(dpart.at[h], p, plus, minus, rp1.at[h], rp2.at[h], ra.at[h],
                               rb.at[h], sm1.at[h], sm2.at[h], started[h]))

    ag = []
    for h in range(2):
        for f in fourth[h]:
            f.wait_recv()
        acc = jnp.zeros((192, 256), F32)
        for a in range(3):
            rows, lanes = pl.ds((2 - a) * 128, 256), pl.ds(h * HALF, HALF)
            wa = jnp.concatenate([wx[h, j, a] for j in range(4)], axis=0)
            for g in (ghi, glo):
                acc = acc + lax.dot_general(wa, g[rows, lanes], (((1,), (1,)), ((), ())),
                                            preferred_element_type=F32)
        ag.append(acc)
    for m in range(16):
        perm_scr[12 * m:12 * m + 12, :] = ag[1][12 * ((m % 4) * 4 + m // 4):12 * ((m % 4) * 4 + m // 4) + 12]
    norm_grad = (ag[0] + perm_scr[...]) * slope
    tot2 = group_sums(norm_grad, norm_grad * normed)
    s2 = stats_start(1, tot2)

    second_rs = []
    for h in range(2):
        p = rs_places[h][0]
        whole = reduce_end(dpart.at[h], p, ra.at[h], rb.at[h], started[h], mids[h])
        for j in range(4):
            dpart2[h, j, :, 8:16] = jnp.zeros((3, 8, HALF), F32)
            for a in range(3):
                dpart2[h, j, a, 0:12] = whole[a, 12 * j:12 * j + 12]
        p2, plus2, minus2 = rs_places[h][3:]
        second_rs.append(reduce_start(dpart2.at[h], sb2.at[h], p2, plus2, minus2,
                                      rq1.at[h], rq2.at[h], ra2.at[h], rb2.at[h]))
    mids2 = []
    for h in range(2):
        p2, plus2, minus2 = rs_places[h][3:]
        mids2.append(reduce_mid(dpart2.at[h], p2, plus2, minus2, rq1.at[h], rq2.at[h], ra2.at[h],
                                rb2.at[h], sn1.at[h], sn2.at[h], second_rs[h]))

    tot2 = stats_end(1, tot2, s2)
    mean2 = tot2[0:4] / n_norm
    d = inv * (norm_grad - wide(mean2[0:2]) - normed * wide(mean2[2:4]))
    back = lax.dot_general(d.astype(BF), pick_bf, (((0,), (0,)), ((), ())),
                           preferred_element_type=F32)
    dsend[...] = back.astype(BF).reshape(2, 2, 64, 384)
    c_out = copy(dsend.at[:, 1 - core], drecv, partner)

    fin[42:48] = jnp.zeros((6, 16, 128), F32)
    for h in range(2):
        p2 = rs_places[h][3]
        done = reduce_end(dpart2.at[h], p2, ra2.at[h], rb2.at[h], second_rs[h], mids2[h])
        for a in range(3):
            for k in range(7):
                fin[h * 21 + a * 7 + k] = done[a, :, 128 * k:128 * k + 128]

    zs = []
    for k in range(1, 8):
        owner = lax.rem(z + k, 8)
        zs.append(copy(fin.at[pl.ds(6 * owner, 6)], zin.at[k - 1], column[k - 1]))
    c_out.wait_recv()
    dacts[...] = dsend[:, core] + drecv[...]
    total = fin[pl.ds(6 * z, 6)]
    for k in range(7):
        zs[k].wait_recv()
        total = total + zin[k]
    zred[...] = total
    zg = [copy(zred, zout.at[pl.ds(6 * z, 6)], column[k]) for k in range(7)]
    zout[pl.ds(6 * z, 6)] = total
    for c in zg:
        c.wait_recv()
    dw[...] = zout[0:42]
    for c in copies:
        c.wait_send()


def shards(acts, gamma, beta, weights, cotangent):
    frames, low_rows, low_cols, channels = acts.shape
    n_norm = float(low_rows * 32 * low_cols * (channels // GROUPS))
    acts2 = acts.reshape(2, 64, 384)
    pairs = cotangent.reshape(2, 2, 64, 2, 192)
    cot = jnp.concatenate(
        [pairs[..., 0, :128], pairs[..., 1, :128], pairs[..., 0, 128:], pairs[..., 1, 128:]], -1)
    w9 = weights.reshape(12, 3, 9, 192)
    w = jnp.concatenate(
        [w9[..., :128].reshape(12, 3, 1152), w9[..., 128:].reshape(12, 3, 576),
         jnp.zeros((12, 3, 64), BF)], -1)
    w = jnp.pad(w.reshape(12, 3, 2, HALF).transpose(2, 1, 0, 3), ((0, 0), (0, 0), (0, 4), (0, 0)))
    vm = pl.BlockSpec(memory_space=VMEM)
    dma = pltpu.SemaphoreType.DMA((NCOPY,))
    dacts, dw = pl.pallas_call(
        lambda *refs: kernel(n_norm, *refs),
        out_shape=(jax.ShapeDtypeStruct((2, 64, 384), BF),
                   jax.ShapeDtypeStruct((42, 16, 128), F32)),
        in_specs=[vm] * 5,
        out_specs=(vm, vm),
        scratch_shapes=[
            VMEM((2, 2, 64, 384), BF), VMEM((4, 6, 64, 384), BF),
            VMEM((2, 8, 128), F32), VMEM((2, 15, 8, 128), F32),
            VMEM((512, 1792), BF), VMEM((512, 1792), BF),
            VMEM((2, 4, 3, 16, HALF), BF), VMEM((2, 4, 3, 48, HALF), BF),
            VMEM((2, 4, 3, 48, HALF), F32), VMEM((2, 4, 3, 48, HALF), BF),
            VMEM((2, 3, 48, CUT), BF), VMEM((2, 3, 48, HALF - CUT), BF),
            VMEM((2, 3, 48, HALF), BF), VMEM((2, 3, 48, HALF), BF),
            VMEM((2, 3, 48, CUT), BF), VMEM((2, 3, 48, HALF - CUT), BF),
            VMEM((2, 4, 3, 16, HALF), F32), VMEM((2, 4, 3, 16, HALF), BF),
            VMEM((2, 3, 16, CUT), BF), VMEM((2, 3, 16, HALF - CUT), BF),
            VMEM((2, 3, 16, HALF), BF), VMEM((2, 3, 16, HALF), BF),
            VMEM((2, 3, 16, CUT), BF), VMEM((2, 3, 16, HALF - CUT), BF),
            VMEM((48, 16, 128), F32), VMEM((8, 128), F32), VMEM((7, 6, 16, 128), F32),
            VMEM((6, 16, 128), F32), VMEM((48, 16, 128), F32),
            VMEM((2, 2, 64, 384), BF), VMEM((2, 64, 384), BF), VMEM((192, 256), F32),
            dma, dma,
        ],
        compiler_params=pltpu.CompilerParams(
            collective_id=0, has_side_effects=True, vmem_limit_bytes=60 * 1024 * 1024),
        name="backward",
    )(acts2, cot, w, gamma.reshape(1, 384), beta.reshape(1, 384))
    flat = dw.reshape(2, 3, 7, 16, 128)[:, :, :, :12].transpose(3, 1, 0, 2, 4).reshape(12, 3, 1792)
    low = flat[..., :1152].reshape(12, 3, 9, 128)
    high = flat[..., 1152:1728].reshape(12, 3, 9, 64)
    d_weights = jnp.concatenate([low, high], -1).reshape(12, 27, 192)
    return dacts.reshape(2, 1, 64, 384), d_weights


def solution(mesh):
    placed = (
        P("block", "tile", None, None),
        P(),
        P(),
        P("tile", None, None),
        P("block", "tile", None, None),
    )
    return jax.shard_map(
        shards,
        mesh=mesh,
        in_specs=placed,
        out_specs=(P("block", "tile", None, None), P("tile", None, None)),
        check_vma=False,
    )
```

time: 433 us -> 78.1 us (0.18)
  waiting for transfers between devices: 147 us -> 0 us
  blocking collectives: 109 us -> 0 us
  local copies, waits for them, and re-layouts: 102 us -> 7.02 us
  Pallas kernels: 0 us -> 67.5 us
  matrix products: 33.4 us -> 0 us
  starting transfers between devices: 20.7 us -> 0 us
  between operations: 14.2 us -> 0.81 us
    psum x2 -> x0, blocking collectives: 109 us -> none  [the longest x1 56.1 us: shards(): stat_sum, stat_sq = lax.psum((stat_sum, stat_sq), 'tile')]
    psum x1 -> x0, waiting for transfers between devices: 74.3 us -> none  [shards(): whole_terms = lax.psum(whole_terms, 'block')]
    pallas_call x0 -> x1, Pallas kernels: none -> 67.5 us  [shards(): pl.pallas_call(lambda *refs: kernel(n_norm, *refs), out_shape=(jax.ShapeD...]
    reduce_scatter x1 -> x0, waiting for transfers between devices: 60.6 us -> none  [shards(): lax.psum_scatter(whole_terms, 'tile', scatter_dimension=0, tiled=True)]
    concatenate x29 -> x3, local copies, waits for them, and re-layouts: 34.5 us -> 0.3 us  [the longest x2 0.21 us: shards(): d_weights = jnp.concatenate([low, high], -1).reshape(12, 27, 192)]
    dot_general x28 -> x0, matrix products: 33.4 us -> none  [the longest x27 26.7 us: shards(): lax.dot_general(window_h, flat_grads, (((0,), (0,)), ((), ())), preferred...]
    slice x28 -> x10, local copies, waits for them, and re-layouts: 33.5 us -> 0.46 us  [the longest x2 0.1 us: shards(): low = flat[..., :1152].reshape(12, 3, 9, 128)]
    ppermute x6 -> x0, starting transfers between devices: 20.5 us -> none  [the longest x2 10.8 us: padded_2(): after = lax.ppermute(first, axis, down)]
  transfers between devices with their start and end apart: 9 -> 0, of which waited for: 7 -> 0; matrix products, arithmetic and copies ran while one was open for 17% -> 0% of each run, Pallas kernels for 0% -> 0%
where the time goes in v1:
time: 78.1 us; the launch traced here: 76.9 us
  Pallas kernels  67.5 us (86%)
  local copies, waits for them, and re-layouts  7.02 us (9%)
  other arithmetic  1.55 us (2%)
  between operations  0.81 us (1%)
    pallas_call x1, Pallas kernels, shards(): pl.pallas_call(lambda *refs: kernel(n_norm, *refs), out_shape=(jax.ShapeD...  67.5 us
    unnamed x10, local copies, waits for them, and re-layouts  3.34 us

profile of v1, /device:TPU:2, one launch (start us, length us, event | category | flops | bytes accessed | tf_op | source)
XLA Modules:
  0.0 76.9 jit_solution(11325555626402091657)
XLA Ops:
  0.6 0.0 copy-start.2
  0.6 1.3 %reshape.50.refs_3_ = f32[1,384]{1,0:T(1,128)} reshape(f32[384]{0:T(512)} %param.6) | data formatting | bytes 3072 | tf_op jit(solution)/shard_map/reshape | solution.py:381
  1.9 0.0 copy-done.2
  1.9 0.6 reshape.51.refs_4_
  2.5 1.0 %copy.24 = bf16[12,27,192]{2,0,1:T(8,128)(2,1)S(1)} copy(bf16[12,27,192]{2,1,0:T(8,128)(2,1)} %param.8) | data formatting | bytes 248832 | tf_op args[3]
  3.6 0.1 reshape.47
  3.7 0.1 reshape.48
  3.9 0.1 concatenate.15
  4.0 0.1 reshape.49
  4.1 0.0 copy-start
  4.1 0.7 pad.4.refs_2_
  4.8 0.3 copy-done
  5.0 0.2 copy.19
  5.2 0.1 fusion
  5.3 0.1 fusion.1
  5.5 0.8 %pad_maximum_fusion.1.refs_1_ = bf16[2,2,64,384]{3,2,1,0:T(8,128)(2,1)} fusion(bf16[2,2,64,64]{3,2,1,0:T(8,128)(2,1)S(1)} %get-tuple-element.16, bf16[2,2,64,64]{3,2,1,0:T(8,128)(2,1)S(1)} %get-tuple-element.17, bf16[2,2,64,128]{3,2,1,0:T(8,128)(2,1)S(1)} %get-tuple-element.18, bf16[2,2,64,128]{3,2,1,0:T(8,128)(2,1)S(1)} %get-tuple-element.19), kind=kLoop, calls=%fused_computation.2 | loop fusion | flops 786432 | bytes 393216 | tf_op jit(solution)/shard_map/concatenate | solution.py:345
  6.3 67.5 %backward.1 = (bf16[2,64,384]{2,1,0:T(8,128)(2,1)}, f32[42,16,128]{2,1,0:T(8,128)}) custom-call(bf16[2,64,384]{2,1,0:T(8,128)(2,1)} %bitcast.37, bf16[2,2,64,384]{3,2,1,0:T(8,128)(2,1)} %pad_maximum_fusion.1.refs_1_, bf16[2,3,16,896]{3,2,1,0:T(8,128)(2,1)} %pad.4.refs_2_, f32[1,384]{1,0:T(1,128)} %reshape.50.refs_3_, f32[1,384]{1,0:T(1,128)} %reshape.51.refs_4_), custom_call_target="tpu_custom_call" | custom-call | tf_op jit(solution)/shard_map/backward/pallas_call | solution.py:354
  73.8 1.1 %copy.43 = f32[2,3,7,12,128]{4,2,0,3,1:T(8,128)S(1)} copy(f32[2,3,7,12,128]{4,3,2,1,0:T(8,128)} %bitcast.36) | data formatting | bytes 516096
  74.9 0.1 reshape.54
  75.0 0.1 copy.29
  75.1 0.1 concatenate.16
  75.2 0.1 copy.30
  75.2 0.1 concatenate.17
  75.4 0.0 copy-start.1
  75.4 0.8 %pad_maximum_fusion = f32[12,27,192]{2,1,0:T(8,128)} fusion(f32[12,27,64]{2,1,0:T(8,128)S(1)} %concatenate.17, f32[12,27,128]{2,1,0:T(8,128)S(1)} %concatenate.16), kind=kLoop, calls=%fused_computation | loop fusion | flops 62208 | bytes 497664 | tf_op jit(solution)/shard_map/concatenate | solution.py:385
  76.1 0.1 copy-done.1
  76.2 0.6 copy.46
  (10 shorter events, 0.2 us)
Async XLA Ops:
  0.6 1.3 %copy-start.2 = (f32[384]{0:T(512)S(1)}, f32[384]{0:T(512)}, u32[]{:S(2)}) copy-start(f32[384]{0:T(512)} %param.7) | copy-start | bytes 4612
  4.1 1.0 %copy-start = (bf16[2,2,128,192]{2,3,1,0:T(8,128)(2,1)S(1)}, bf16[2,2,128,192]{2,3,1,0:T(8,128)(2,1)}, u32[]{:S(2)}) copy-start(bf16[2,2,128,192]{2,3,1,0:T(8,128)(2,1)} %param.9) | copy-start | bytes 589828
  75.4 0.9 %copy-start.1 = (bf16[2,64,384]{2,1,0:T(8,128)(2,1)S(1)}, bf16[2,64,384]{2,1,0:T(8,128)(2,1)}, u32[]{:S(2)}) copy-start(bf16[2,64,384]{2,1,0:T(8,128)(2,1)} %get-tuple-element.4) | copy-start | bytes 294916

commit v2 on v1

v2 whole, which is shorter than its diff:
```python
import jax
import jax.numpy as jnp
from jax import lax
from jax.experimental import pallas as pl
from jax.experimental.pallas import tpu as pltpu
from jax.sharding import PartitionSpec as P

GROUPS = 32
NORM_EPS = 1e-06
MESH = pl.DeviceIdType.MESH
BF = jnp.bfloat16
F32 = jnp.float32
VMEM = pltpu.VMEM
NCOPY = 110
TAPK = 896
LANES = (1408, 1280)
CUTS = (768, 640)
SEGMENTS = (((0, 0, 896, 0), (1, 0, 512, 896)), ((1, 512, 384, 0), (2, 0, 896, 384)))


def iota(shape, dim):
    return lax.broadcasted_iota(jnp.int32, shape, dim)


def div12(v):
    return (v * 5462) >> 16


def kernel(n_norm, acts, cot, w, gamma, beta, dacts, dw,
           actbuf, cotbuf, stat_out, stat_in, ghi, glo, hbuf, hswap,
           wy0, wy1, wx0, wx1, dp0, dp1, sb0, sb1,
           r10, r11, r20, r21, ra0, ra1, rb0, rb1, sm0, sm1, sn0, sn1,
           ep0, ep1, eb0, eb1, q10, q11, q20, q21, ea0, ea1, ec0, ec1, tm0, tm1, tn0, tn1,
           fin, zin, zred, zout, actp, actin, perm_scr, dsend, drecv, send_sem, recv_sem):
    z = lax.axis_index("block")
    tile = lax.axis_index("tile")
    core = lax.rem(tile, 2)
    q = lax.div(tile, 2)
    y = lax.rem(q, 4)
    x = lax.div(q, 4)
    u = lax.rem(z, 2)
    pair = lax.div(z, 2)
    wy, wx = (wy0, wy1), (wx0, wx1)

    def chip(cx, cy):
        return {"tile": (cx * 4 + cy) * 2 + core}

    partner = {"tile": tile + 1 - 2 * core}
    outer = {"tile": lax.rem(tile + 2 * core - 1 + 32, 32)}
    xp, xm = chip(lax.rem(x + 1, 4), y), chip(lax.rem(x + 3, 4), y)
    yp, ym = chip(x, lax.rem(y + 1, 4)), chip(x, lax.rem(y + 3, 4))
    plane = [{"tile": lax.rem(q + d, 16) * 2 + core} for d in range(1, 16)]
    column = [{"block": lax.rem(z + k, 8)} for k in range(1, 8)]
    twin = {"block": z + 1 - 2 * u}

    copies = []
    count = [0]

    def make(src, dst, device, slot=None):
        k = count[0]
        count[0] += 1
        return pltpu.make_async_remote_copy(
            src_ref=src, dst_ref=dst, send_sem=send_sem.at[k],
            recv_sem=recv_sem.at[k if slot is None else slot],
            device_id=device, device_id_type=MESH)

    def copy(src, dst, device):
        c = make(src, dst, device)
        copies.append(c)
        c.start()
        return c

    barrier = pltpu.get_barrier_semaphore()
    friends = plane + column + [partner, outer]
    for dev in friends:
        pl.semaphore_signal(barrier, inc=1, device_id=dev, device_id_type=MESH)
    pl.semaphore_wait(barrier, len(friends))

    own = pl.ds(1 + 2 * core, 2)
    mine, theirs, later = pl.ds(2 * u, 2), pl.ds(2 - 2 * u, 2), pl.ds(4, 2)
    half = pl.ds(pl.multiple_of(96 * u, 32), 96)
    other_half = pl.ds(pl.multiple_of(96 - 96 * u, 32), 96)
    line, there = 5 * core, 5 * (1 - core)
    c_act = copy(acts, actbuf.at[:, core], partner)
    c_twin = copy(cot.at[:, :, other_half], cotbuf.at[mine, own], twin)
    slot = count[0]
    c_next1 = make(cot.at[:, :, pl.ds(0, 96)], cotbuf.at[later, own], column[5], slot)
    c_next2 = make(cot.at[:, :, pl.ds(96, 96)], cotbuf.at[later, own], column[6], slot)

    @pl.when(u == 0)
    def _():
        c_next1.start()
        c_next2.start()

    c_pair = copy(cot.at[:, :, half], cotbuf.at[mine, own], partner)
    c_edge = copy(cot.at[:, core, half], cotbuf.at[mine, there], outer)

    places = ((y, yp, ym, x, xp, xm), (x, xp, xm, y, yp, ym))

    def gather_start(buf, p, plus, minus):
        return copy(buf.at[p], buf.at[p], plus), copy(buf.at[p], buf.at[p], minus)

    def gather_forward(h, buf, p, plus, minus, pair_):
        lo, hi = pl.ds(0, CUTS[h]), pl.ds(CUTS[h], LANES[h] - CUTS[h])
        pair_[0].wait_recv()
        low = lax.rem(p + 3, 4)
        f1 = copy(buf.at[low, :, lo], buf.at[low, :, lo], plus)
        pair_[1].wait_recv()
        high = lax.rem(p + 1, 4)
        f2 = copy(buf.at[high, :, hi], buf.at[high, :, hi], minus)
        return f1, f2

    first = []
    for h in range(2):
        p, plus, minus = places[h][:3]
        wy[h][p] = w[u, :, 1408 * h:1408 * h + LANES[h]]
        first.append(gather_start(wy[h], p, plus, minus))

    actbuf[:, core] = acts[...]
    cotbuf[mine, own] = cot[:, :, half, :]
    blk = div12(iota((192, 384), 0))
    pick = iota((192, 384), 1) == iota((192, 384), 0) + 12 * blk + 12 * core
    pick_bf = jnp.where(pick, 1.0, 0.0).astype(BF)
    gcol = jnp.sum(jnp.where(pick, gamma[...][None, :], 0.0), axis=1, keepdims=True)
    bcol = jnp.sum(jnp.where(pick, beta[...][None, :], 0.0), axis=1, keepdims=True)
    member = iota((192, 128), 1) == div12(iota((192, 128), 0))
    c_act.wait_recv()
    xt = lax.dot_general(pick_bf, actbuf[...].reshape(256, 384), (((1,), (1,)), ((), ())),
                         preferred_element_type=F32)

    def group_sums(a, b):
        lines = []
        for value in (a, b):
            for t in range(2):
                c = jnp.sum(value[:, 128 * t:128 * t + 128], axis=1, keepdims=True)
                lines.append(jnp.sum(jnp.where(member, c, 0.0), axis=0, keepdims=True))
        return jnp.concatenate(lines + [jnp.zeros((4, 128), F32)], axis=0)

    def spread(v):
        return jnp.sum(jnp.where(member, v, 0.0), axis=1, keepdims=True)

    def stats_start(k, total):
        stat_out[k] = total
        return [copy(stat_out.at[k], stat_in.at[k, d], plane[d]) for d in range(15)]

    def stats_end(k, total, cs):
        for d in range(15):
            cs[d].wait_recv()
            total = total + stat_in[k, d]
        return total

    tot1 = group_sums(xt, xt * xt)
    s1 = stats_start(0, tot1)

    def pass_edge(frames, c):
        c.wait_recv()
        return copy(cotbuf.at[frames, line], cotbuf.at[frames, line], partner)

    def pass_rows(frames):
        return (copy(cotbuf.at[frames, own], cotbuf.at[frames, own], partner),
                copy(cotbuf.at[frames, 1 + 3 * core], cotbuf.at[frames, there], outer))

    cot_waits = [c_pair]
    second = [gather_forward(h, wy[h], *places[h][:3], first[h]) for h in range(2)]
    cot_waits.append(pass_edge(mine, c_edge))
    c_twin.wait_recv()
    rows1, edge1 = pass_rows(theirs)
    c_next1.wait_recv()
    rows2, edge2 = pass_rows(later)

    third = []
    for h in range(2):
        for f in second[h]:
            f.wait_recv()
        p2, plus2, minus2 = places[h][3:]
        parts = [wy[h][j].astype(F32)[0:12] for j in range(4)]
        wx[h][p2] = jnp.concatenate(parts, axis=0).astype(BF)
        third.append(gather_start(wx[h], p2, plus2, minus2))

    tot1 = stats_end(0, tot1, s1)
    mean_l = tot1[0:2] / n_norm
    inv_l = lax.rsqrt(tot1[2:4] / n_norm - mean_l * mean_l + NORM_EPS)
    wide = lambda m: jnp.concatenate(
        [jnp.broadcast_to(spread(m[t:t + 1]), (192, 128)) for t in range(2)], axis=1)
    inv = wide(inv_l)
    normed = (xt - wide(mean_l)) * inv
    shifted = normed * gcol + bcol
    gate = jax.nn.sigmoid(shifted)
    hidden = (shifted * gate).astype(BF)
    hbuf[u] = hidden
    c_hid = copy(hbuf.at[u], hbuf.at[u], twin)
    slope = gate * (1.0 + shifted * (1.0 - gate)) * gcol
    b2 = div12(iota((192, 192), 0))
    swap = iota((192, 192), 1) == iota((192, 192), 0) + 12 * ((b2 & 3) * 4 + (b2 >> 2) - b2)
    swap_bf = jnp.where(swap, 1.0, 0.0).astype(BF)
    hswap[u] = jnp.dot(swap_bf, hidden, preferred_element_type=F32).astype(BF)

    cot_waits.append(pass_edge(theirs, edge1))
    cot_waits.append(pass_edge(later, edge2))
    for c in cot_waits + [rows1, rows2]:
        c.wait_recv()
    left = iota((96, 128), 1) < 64
    col, lane = iota((128, 384), 0), iota((128, 384), 1)
    shift = col - 2 * (lane & 63) + (lane >> 7) - 1
    summer = jnp.where((shift == 0) | (shift == 1), 1.0, 0.0).astype(BF)
    ghi[864:896] = jnp.zeros((32, 768), BF)
    glo[864:896] = jnp.zeros((32, 768), BF)
    for f in range(6):
        sums = jnp.dot(cotbuf[f].reshape(576, 128), summer, preferred_element_type=F32)
        if f >= 4:
            sums = jnp.where(pair < 3, sums, 0.0)
        lines = [sums[96 * h:96 * h + 96] for h in range(6)]
        lines[0] = jnp.where(q > 0, lines[0], 0.0)
        lines[5] = jnp.where(q < 15, lines[5], 0.0)
        for e in range(3):
            ls = [v[:, 128 * e:128 * e + 128] for v in lines]
            for b in range(3):
                v = jnp.where(left, ls[2 - b] + ls[3 - b], ls[4 - b] + ls[5 - b])
                hi = v.astype(BF)
                k = (3 * b + e) * 96
                ghi[k:k + 96, 128 * f:128 * f + 128] = hi
                glo[k:k + 96, 128 * f:128 * f + 128] = (v - hi.astype(F32)).astype(BF)

    fourth = [gather_forward(h, wx[h], *places[h][3:], third[h]) for h in range(2)]

    def reduce_start(h, part, sbuf, p, plus, minus, r1, r2, a_in, b_in):
        opp, nxt, prv = lax.rem(p + 2, 4), lax.rem(p + 1, 4), lax.rem(p + 3, 4)
        lo, hi = pl.ds(0, CUTS[h]), pl.ds(CUTS[h], LANES[h] - CUTS[h])
        sbuf[opp] = part[opp].astype(BF)
        o1 = copy(sbuf.at[opp, :, lo], r1, plus)
        o2 = copy(sbuf.at[opp, :, hi], r2, minus)
        sbuf[nxt] = part[nxt].astype(BF)
        n1 = copy(sbuf.at[nxt, :, hi], a_in.at[:, hi], plus)
        sbuf[prv] = part[prv].astype(BF)
        n2 = copy(sbuf.at[prv, :, lo], b_in.at[:, lo], minus)
        return o1, o2, n1, n2

    def reduce_mid(h, part, p, plus, minus, r1, r2, a_in, b_in, s_1, s_2, cs):
        nxt, prv = lax.rem(p + 1, 4), lax.rem(p + 3, 4)
        lo, hi = pl.ds(0, CUTS[h]), pl.ds(CUTS[h], LANES[h] - CUTS[h])
        cs[0].wait_recv()
        s_1[...] = (part[nxt, :, lo] + r1[...].astype(F32)).astype(BF)
        m1 = copy(s_1, a_in.at[:, lo], plus)
        cs[1].wait_recv()
        s_2[...] = (part[prv, :, hi] + r2[...].astype(F32)).astype(BF)
        m2 = copy(s_2, b_in.at[:, hi], minus)
        return m1, m2

    def reduce_end(part, p, a_in, b_in, cs, ms):
        for c in (cs[2], cs[3], ms[0], ms[1]):
            c.wait_recv()
        return part[p] + a_in[...].astype(F32) + b_in[...].astype(F32)

    rs_places = (places[1], places[0])
    hid = (hbuf, hswap)
    dp, sb = (dp0, dp1), (sb0, sb1)
    rs_in = ((r10, r20, ra0, rb0), (r11, r21, ra1, rb1))
    rs_mid = ((sm0, sn0), (sm1, sn1))

    def partial(h, v):
        outs = []
        for a, k0, rows, _ in SEGMENTS[h]:
            lanes = pl.ds(pl.multiple_of(256 * v + (2 - a) * 128, 128), 256)
            acc = None
            for g in (ghi, glo):
                d = lax.dot_general(hid[h][v], g[k0:k0 + rows, lanes], (((1,), (1,)), ((), ())),
                                    preferred_element_type=F32)
                acc = d if acc is None else acc + d
            outs.append(acc)
        return outs

    for h in range(2):
        for (a, k0, rows, l0), d in zip(SEGMENTS[h], partial(h, u)):
            for j in range(4):
                dp[h][j, :, l0:l0 + rows] = d[48 * j:48 * j + 48]
    c_hid.wait_recv()
    hswap[1 - u] = jnp.dot(swap_bf, hbuf[1 - u], preferred_element_type=F32).astype(BF)
    started = []
    for h in range(2):
        for (a, k0, rows, l0), d in zip(SEGMENTS[h], partial(h, 1 - u)):
            for j in range(4):
                dp[h][j, :, l0:l0 + rows] += d[48 * j:48 * j + 48]
        p, plus, minus = rs_places[h][:3]
        started.append(reduce_start(h, dp[h], sb[h], p, plus, minus, *rs_in[h]))

    ag = []
    for h in range(2):
        for f in fourth[h]:
            f.wait_recv()
        acc = jnp.zeros((192, 512), F32)
        for a, k0, rows, l0 in SEGMENTS[h]:
            wa = jnp.concatenate([wx[h][j, :, l0:l0 + rows] for j in range(4)], axis=0)
            for g in (ghi, glo):
                acc = acc + jnp.dot(wa, g[k0:k0 + rows, (2 - a) * 128:(2 - a) * 128 + 512],
                                    preferred_element_type=F32)
        ag.append(acc)
    for m in range(16):
        b = (m % 4) * 4 + m // 4
        perm_scr[12 * m:12 * m + 12, :] = ag[1][12 * b:12 * b + 12]
    for v in range(2):
        actp[v] = ag[0][:, 256 * v:256 * v + 256] + perm_scr[:, 256 * v:256 * v + 256]
    c_grad = copy(actp.at[1 - u], actin, twin)

    mids = []
    for h in range(2):
        p, plus, minus = rs_places[h][:3]
        mids.append(reduce_mid(h, dp[h], p, plus, minus, *rs_in[h], *rs_mid[h], started[h]))

    c_grad.wait_recv()
    norm_grad = (actp[u] + actin[...]) * slope
    tot2 = group_sums(norm_grad, norm_grad * normed)
    s2 = stats_start(1, tot2)

    ep, eb = (ep0, ep1), (eb0, eb1)
    rs_in2 = ((q10, q20, ea0, ec0), (q11, q21, ea1, ec1))
    rs_mid2 = ((tm0, tn0), (tm1, tn1))
    second_rs = []
    for h in range(2):
        p = rs_places[h][0]
        whole = reduce_end(dp[h], p, rs_in[h][2], rs_in[h][3], started[h], mids[h])
        for j in range(4):
            ep[h][j, 8:16] = jnp.zeros((8, LANES[h]), F32)
            ep[h][j, 0:12] = whole[12 * j:12 * j + 12]
        p2, plus2, minus2 = rs_places[h][3:]
        second_rs.append(reduce_start(h, ep[h], eb[h], p2, plus2, minus2, *rs_in2[h]))
    mids2 = []
    for h in range(2):
        p2, plus2, minus2 = rs_places[h][3:]
        mids2.append(reduce_mid(h, ep[h], p2, plus2, minus2, *rs_in2[h], *rs_mid2[h],
                                second_rs[h]))

    tot2 = stats_end(1, tot2, s2)
    mean2 = tot2[0:4] / n_norm
    d = inv * (norm_grad - wide(mean2[0:2]) - normed * wide(mean2[2:4]))
    back = lax.dot_general(d.astype(BF), pick_bf, (((0,), (0,)), ((), ())),
                           preferred_element_type=F32)
    dsend[...] = back.astype(BF).reshape(2, 2, 64, 384)
    c_out = copy(dsend.at[:, 1 - core], drecv, partner)

    rest = []
    for h in range(2):
        p2 = rs_places[h][3]
        done = reduce_end(ep[h], p2, rs_in2[h][2], rs_in2[h][3], second_rs[h], mids2[h])
        for k in range(LANES[h] // 128):
            fin[11 * h + k] = done[0:8, 128 * k:128 * k + 128]
            rest.append(done[8:12, 128 * k:128 * k + 128])
    rest.append(jnp.zeros((4, 128), F32))
    for m in range(11):
        fin[21 + m] = jnp.concatenate([rest[2 * m], rest[2 * m + 1]], axis=0)

    zs = []
    for m in range(1, 4):
        owner = lax.rem(pair + m, 4)
        zs.append(copy(fin.at[pl.ds(8 * owner, 8)], zin.at[m - 1], column[2 * m - 1]))
    c_out.wait_recv()
    dacts[...] = dsend[:, core] + drecv[...]
    total = fin[pl.ds(8 * pair, 8)]
    for m in range(3):
        zs[m].wait_recv()
        total = total + zin[m]
    zred[...] = total
    zg = [copy(zred, zout.at[u, pl.ds(8 * pair, 8)], column[k]) for k in range(7)]
    zout[u, pl.ds(8 * pair, 8)] = total
    for c in zg:
        c.wait_recv()
    dw[...] = zout[...]
    for c in copies:
        c.wait_send()

    @pl.when(u == 0)
    def _():
        c_next1.wait_send()
        c_next2.wait_send()


def shards(acts, gamma, beta, weights, cotangent):
    frames, low_rows, low_cols, channels = acts.shape
    n_norm = float(low_rows * 32 * low_cols * (channels // GROUPS))
    acts2 = acts.reshape(2, 64, 384)
    cot = cotangent.swapaxes(2, 3)
    w = weights.reshape(12, 3, 9, 2, 96).transpose(3, 0, 1, 2, 4).reshape(2, 12, 3, 864)
    w = jnp.pad(w, ((0, 0), (0, 4), (0, 0), (0, 32))).reshape(2, 16, 3 * TAPK)
    vm = pl.BlockSpec(memory_space=VMEM)
    dma = pltpu.SemaphoreType.DMA((NCOPY,))
    both = lambda lead, dtype, lanes=LANES: [VMEM((*lead, n), dtype) for n in lanes]
    tails = tuple(n - c for n, c in zip(LANES, CUTS))

    def ring(rows):
        return (both((4, rows), F32) + both((4, rows), BF) + both((rows,), BF, CUTS)
                + both((rows,), BF, tails) + both((rows,), BF) + both((rows,), BF)
                + both((rows,), BF, CUTS) + both((rows,), BF, tails))

    dacts, dw = pl.pallas_call(
        lambda *refs: kernel(n_norm, *refs),
        out_shape=(jax.ShapeDtypeStruct((2, 64, 384), BF),
                   jax.ShapeDtypeStruct((2, 32, 8, 128), F32)),
        in_specs=[vm] * 5,
        out_specs=(vm, vm),
        scratch_shapes=[
            VMEM((2, 2, 64, 384), BF), VMEM((6, 6, 96, 128), BF),
            VMEM((2, 8, 128), F32), VMEM((2, 15, 8, 128), F32),
            VMEM((TAPK, 768), BF), VMEM((TAPK, 768), BF),
            VMEM((2, 192, 256), BF), VMEM((2, 192, 256), BF),
            *both((4, 16), BF), *both((4, 48), BF), *ring(48), *ring(16),
            VMEM((32, 8, 128), F32), VMEM((3, 8, 8, 128), F32), VMEM((8, 8, 128), F32),
            VMEM((2, 32, 8, 128), F32),
            VMEM((2, 192, 256), F32), VMEM((192, 256), F32), VMEM((192, 512), F32),
            VMEM((2, 2, 64, 384), BF), VMEM((2, 64, 384), BF),
            dma, dma,
        ],
        compiler_params=pltpu.CompilerParams(
            collective_id=0, has_side_effects=True, vmem_limit_bytes=60 * 1024 * 1024),
        name="backward",
    )(acts2, cot, w, gamma, beta)
    top = dw[:, :21]
    rest = dw[:, 21:].reshape(2, 22, 4, 128)[:, :21]
    flat = jnp.concatenate([top, rest], 2).reshape(2, 3, 7, 12, 128)
    flat = flat.transpose(3, 1, 0, 2, 4).reshape(12, 3, 2, TAPK)[..., :864]
    d_weights = flat.reshape(12, 3, 2, 9, 96).transpose(0, 1, 3, 2, 4).reshape(12, 27, 192)
    return dacts.reshape(2, 1, 64, 384), d_weights


def solution(mesh):
    placed = (
        P("block", "tile", None, None),
        P(),
        P(),
        P("tile", None, None),
        P("block", "tile", None, None),
    )
    return jax.shard_map(
        shards,
        mesh=mesh,
        in_specs=placed,
        out_specs=(P("block", "tile", None, None), P("tile", None, None)),
        check_vma=False,
    )
```

time: 78.1 us -> 62.9 us (0.81)
  Pallas kernels: 67.5 us -> 55.1 us
  other arithmetic: 1.55 us -> 0.03 us
    pallas_call x1, Pallas kernels: 67.5 us -> 55.1 us  [shards(): pl.pallas_call(lambda *refs: kernel(n_norm, *refs), out_shape=(jax.ShapeD...]
    unnamed x10 -> x4, local copies, waits for them, and re-layouts: 3.34 us -> 0.71 us
    reshape x7 -> x8, local copies, waits for them, and re-layouts: 2.17 us -> 3.73 us  [the longest x3 1.39 us: shards(): weights.reshape(12, 3, 9, 2, 96).transpose(3, 0, 1, 2, 4)]
    concatenate x2 -> x1, other arithmetic: 1.55 us -> 0.03 us  [shards(): flat = jnp.concatenate([top, rest], 2).reshape(2, 3, 7, 12, 128)]
    slice x10 -> x3, local copies, waits for them, and re-layouts: 0.46 us -> 1.84 us  [the longest x1 0.93 us: shards(): top = dw[:, :21]]
where the time goes in v2:
time: 62.9 us; the launch traced here: 62.3 us
  Pallas kernels  55.1 us (88%)
  local copies, waits for them, and re-layouts  6.53 us (10%)
  between operations  0.73 us (1%)
    pallas_call x1, Pallas kernels, shards(): pl.pallas_call(lambda *refs: kernel(n_norm, *refs), out_shape=(jax.ShapeD...  55.1 us
    reshape x3, local copies, waits for them, and re-layouts, shards(): weights.reshape(12, 3, 9, 2, 96).transpose(3, 0, 1, 2, 4)  1.39 us
    reshape x2, local copies, waits for them, and re-layouts, shards(): flat.reshape(12, 3, 2, 9, 96).transpose(0, 1, 3, 2, 4).reshape(12, 27, 192)  1.28 us

profile of v2, /device:TPU:2, one launch (start us, length us, event | category | flops | bytes accessed | tf_op | source)
XLA Modules:
  0.0 62.3 jit_solution(11485540730355085083)
XLA Ops:
  0.6 1.1 %reshape.35 = bf16[12,3,9,2,96]{4,3,2,1,0:T(2,128)(2,1)S(1)} reshape(bf16[12,27,192]{2,1,0:T(8,128)(2,1)} %param.8) | data formatting | bytes 248832 | tf_op jit(solution)/shard_map/reshape | solution.py:381
  1.8 0.3 reshape.36
  2.0 0.1 copy.18
  2.1 0.1 pad.4.clone
  2.2 0.8 %reshape.37.refs_2_ = bf16[2,16,2688]{2,1,0:T(8,128)(2,1)} reshape(bf16[2,16,3,896]{3,2,1,0:T(4,128)(2,1)S(1)} %pad.4.clone) | data formatting | bytes 344064 | tf_op jit(solution)/shard_map/reshape | solution.py:382
  3.0 55.1 %backward.1 = (bf16[2,64,384]{2,1,0:T(8,128)(2,1)}, f32[2,32,8,128]{3,2,1,0:T(8,128)}) custom-call(bf16[2,64,384]{2,1,0:T(8,128)(2,1)} %bitcast.24, bf16[2,2,192,128]{3,2,1,0:T(8,128)(2,1)} %bitcast.23, bf16[2,16,2688]{2,1,0:T(8,128)(2,1)} %reshape.37.refs_2_, f32[384]{0:T(512)} %refs_3_.1, f32[384]{0:T(512)} %refs_4_.1), custom_call_target="tpu_custom_call" | custom-call | tf_op jit(solution)/shard_map/backward/pallas_call | solution.py:393
  58.1 0.9 %slice.13 = f32[2,11,8,128]{3,2,1,0:T(8,128)S(1)} slice(f32[2,32,8,128]{3,2,1,0:T(8,128)} %get-tuple-element.5), slice={[0:2], [21:32], [0:8], [0:128]} | slice | bytes 180224 | tf_op jit(solution)/shard_map/slice | solution.py:416
  59.0 0.9 %slice.12 = f32[2,21,8,128]{3,2,1,0:T(8,128)S(1)} slice(f32[2,32,8,128]{3,2,1,0:T(8,128)} %get-tuple-element.5), slice={[0:2], [0:21], [0:8], [0:128]} | slice | bytes 344064 | tf_op jit(solution)/shard_map/slice | solution.py:415
  60.0 0.1 copy.21
  60.1 0.1 reshape.41
  60.2 0.3 reshape.42
  60.5 0.2 copy.16
  60.7 0.0 copy-start
  60.7 1.0 %reshape.43 = f32[12,27,192]{2,1,0:T(8,128)} reshape(f32[12,3,9,2,96]{4,3,2,1,0:T(2,128)S(1)} %copy.16) | data formatting | bytes 497664 | tf_op jit(solution)/shard_map/reshape | solution.py:419
  61.7 0.0 copy-done
  61.7 0.6 %copy.24 = bf16[2,1,64,384]{3,2,1,0:T(8,128)(2,1)} copy(bf16[2,1,64,384]{3,2,1,0:T(8,128)(2,1)S(1)} %bitcast.25) | data formatting | bytes 196608
  (3 shorter events, 0.1 us)
Async XLA Ops:
  60.7 1.0 %copy-start = (bf16[2,64,384]{2,1,0:T(8,128)(2,1)S(1)}, bf16[2,64,384]{2,1,0:T(8,128)(2,1)}, u32[]{:S(2)}) copy-start(bf16[2,64,384]{2,1,0:T(8,128)(2,1)} %get-tuple-element.4) | copy-start | bytes 294916

commit v3 on v2

--- a/solution.py
+++ b/solution.py
@@ -27,7 +27,7 @@
 
 
 def kernel(n_norm, acts, cot, w, gamma, beta, dacts, dw,
-           actbuf, cotbuf, stat_out, stat_in, ghi, glo, hbuf, hswap,
+           actbuf, cotbuf, stat_out, stat_in, ghi, glo, hbuf, hswap, wflat, dflat,
            wy0, wy1, wx0, wx1, dp0, dp1, sb0, sb1,
            r10, r11, r20, r21, ra0, ra1, rb0, rb1, sm0, sm1, sn0, sn1,
            ep0, ep1, eb0, eb1, q10, q11, q20, q21, ea0, ea1, ec0, ec1, tm0, tm1, tn0, tn1,
@@ -82,15 +82,20 @@
     other_half = pl.ds(pl.multiple_of(96 - 96 * u, 32), 96)
     line, there = 5 * core, 5 * (1 - core)
     c_act = copy(acts, actbuf.at[:, core], partner)
-    c_twin = copy(cot.at[:, :, other_half], cotbuf.at[mine, own], twin)
-    slot = count[0]
-    c_next1 = make(cot.at[:, :, pl.ds(0, 96)], cotbuf.at[later, own], column[5], slot)
-    c_next2 = make(cot.at[:, :, pl.ds(96, 96)], cotbuf.at[later, own], column[6], slot)
-
-    @pl.when(u == 0)
-    def _():
-        c_next1.start()
-        c_next2.start()
+    edge_row, inner_row = 1 + 3 * core, 2 + core
+    nexts, c_twin, c_next = [], [], []
+    for r, dst_row in ((core, edge_row), (1 - core, inner_row)):
+        slot = count[0]
+        c_next.append(make(cot.at[:, r, pl.ds(0, 96)], cotbuf.at[later, dst_row], column[5], slot))
+        nexts.append(c_next[-1])
+        nexts.append(make(cot.at[:, r, pl.ds(96, 96)], cotbuf.at[later, dst_row], column[6], slot))
+
+        @pl.when(u == 0)
+        def _(pair_=nexts[-2:]):
+            for c in pair_:
+                c.start()
+
+        c_twin.append(copy(cot.at[:, r, other_half], cotbuf.at[mine, dst_row], twin))
 
     c_pair = copy(cot.at[:, :, half], cotbuf.at[mine, own], partner)
     c_edge = copy(cot.at[:, core, half], cotbuf.at[mine, there], outer)
@@ -111,9 +116,16 @@
         return f1, f2
 
     first = []
+    wide_w = w[...].astype(F32)
+    wide_w = jnp.where(u == 0, wide_w[..., 0:96], wide_w[..., 96:192])
+    for a in range(3):
+        for b in range(9):
+            k = a * TAPK + 96 * b
+            wflat[0:12, k:k + 96] = wide_w[:, 9 * a + b, :]
+        wflat[0:12, a * TAPK + 864:a * TAPK + TAPK] = jnp.zeros((12, 32), F32)
     for h in range(2):
         p, plus, minus = places[h][:3]
-        wy[h][p] = w[u, :, 1408 * h:1408 * h + LANES[h]]
+        wy[h][p] = wflat[:, 1408 * h:1408 * h + LANES[h]].astype(BF)
         first.append(gather_start(wy[h], p, plus, minus))
 
     actbuf[:, core] = acts[...]
@@ -156,26 +168,19 @@
         c.wait_recv()
         return copy(cotbuf.at[frames, line], cotbuf.at[frames, line], partner)
 
-    def pass_rows(frames):
-        return (copy(cotbuf.at[frames, own], cotbuf.at[frames, own], partner),
-                copy(cotbuf.at[frames, 1 + 3 * core], cotbuf.at[frames, there], outer))
-
-    cot_waits = [c_pair]
+    def pass_row(frames, r, device, to, c):
+        if c is not None:
+            c.wait_recv()
+        return copy(cotbuf.at[frames, r], cotbuf.at[frames, to], device)
+
+    early, late = [c_pair], []
     second = [gather_forward(h, wy[h], *places[h][:3], first[h]) for h in range(2)]
-    cot_waits.append(pass_edge(mine, c_edge))
-    c_twin.wait_recv()
-    rows1, edge1 = pass_rows(theirs)
-    c_next1.wait_recv()
-    rows2, edge2 = pass_rows(later)
-
-    third = []
-    for h in range(2):
-        for f in second[h]:
-            f.wait_recv()
-        p2, plus2, minus2 = places[h][3:]
-        parts = [wy[h][j].astype(F32)[0:12] for j in range(4)]
-        wx[h][p2] = jnp.concatenate(parts, axis=0).astype(BF)
-        third.append(gather_start(wx[h], p2, plus2, minus2))
+    early.append(pass_edge(mine, c_edge))
+    edge1 = pass_row(theirs, edge_row, outer, there, c_twin[0])
+    early.append(pass_row(theirs, edge_row, partner, edge_row, None))
+    edge2 = pass_row(later, edge_row, outer, there, c_next[0])
+    late.append(pass_row(later, edge_row, partner, edge_row, None))
+    early.append(pass_row(theirs, inner_row, partner, inner_row, c_twin[1]))
 
     tot1 = stats_end(0, tot1, s1)
     mean_l = tot1[0:2] / n_norm
@@ -195,9 +200,19 @@
     swap_bf = jnp.where(swap, 1.0, 0.0).astype(BF)
     hswap[u] = jnp.dot(swap_bf, hidden, preferred_element_type=F32).astype(BF)
 
-    cot_waits.append(pass_edge(theirs, edge1))
-    cot_waits.append(pass_edge(later, edge2))
-    for c in cot_waits + [rows1, rows2]:
+    third = []
+    for h in range(2):
+        for f in second[h]:
+            f.wait_recv()
+        p2, plus2, minus2 = places[h][3:]
+        parts = [wy[h][j].astype(F32)[0:12] for j in range(4)]
+        wx[h][p2] = jnp.concatenate(parts, axis=0).astype(BF)
+        third.append(gather_start(wx[h], p2, plus2, minus2))
+
+    early.append(pass_edge(theirs, edge1))
+    late.append(pass_row(later, inner_row, partner, inner_row, c_next[1]))
+    late.append(pass_edge(later, edge2))
+    for c in early:
         c.wait_recv()
     left = iota((96, 128), 1) < 64
     col, lane = iota((128, 384), 0), iota((128, 384), 1)
@@ -206,6 +221,9 @@
     ghi[864:896] = jnp.zeros((32, 768), BF)
     glo[864:896] = jnp.zeros((32, 768), BF)
     for f in range(6):
+        if f == 4:
+            for c in late:
+                c.wait_recv()
         sums = jnp.dot(cotbuf[f].reshape(576, 128), summer, preferred_element_type=F32)
         if f >= 4:
             sums = jnp.where(pair < 3, sums, 0.0)
@@ -306,11 +324,6 @@
         p, plus, minus = rs_places[h][:3]
         mids.append(reduce_mid(h, dp[h], p, plus, minus, *rs_in[h], *rs_mid[h], started[h]))
 
-    c_grad.wait_recv()
-    norm_grad = (actp[u] + actin[...]) * slope
-    tot2 = group_sums(norm_grad, norm_grad * normed)
-    s2 = stats_start(1, tot2)
-
     ep, eb = (ep0, ep1), (eb0, eb1)
     rs_in2 = ((q10, q20, ea0, ec0), (q11, q21, ea1, ec1))
     rs_mid2 = ((tm0, tn0), (tm1, tn1))
@@ -323,6 +336,11 @@
             ep[h][j, 0:12] = whole[12 * j:12 * j + 12]
         p2, plus2, minus2 = rs_places[h][3:]
         second_rs.append(reduce_start(h, ep[h], eb[h], p2, plus2, minus2, *rs_in2[h]))
+    c_grad.wait_recv()
+    norm_grad = (actp[u] + actin[...]) * slope
+    tot2 = group_sums(norm_grad, norm_grad * normed)
+    s2 = stats_start(1, tot2)
+
     mids2 = []
     for h in range(2):
         p2, plus2, minus2 = rs_places[h][3:]
@@ -363,14 +381,26 @@
     zout[u, pl.ds(8 * pair, 8)] = total
     for c in zg:
         c.wait_recv()
-    dw[...] = zout[...]
+    for v in range(2):
+        for k in range(21):
+            dflat[v, 0:8, 128 * k:128 * k + 128] = zout[v, k]
+        for m in range(11):
+            two = zout[v, 21 + m]
+            dflat[v, 8:12, 256 * m:256 * m + 128] = two[0:4]
+            if m < 10:
+                dflat[v, 8:12, 256 * m + 128:256 * m + 256] = two[4:8]
+    for a in range(3):
+        for b in range(9):
+            k = a * TAPK + 96 * b
+            dw[:, 9 * a + b, 0:96] = dflat[0, 0:12, k:k + 96]
+            dw[:, 9 * a + b, 96:192] = dflat[1, 0:12, k:k + 96]
     for c in copies:
         c.wait_send()
 
     @pl.when(u == 0)
     def _():
-        c_next1.wait_send()
-        c_next2.wait_send()
+        for c in nexts:
+            c.wait_send()
 
 
 def shards(acts, gamma, beta, weights, cotangent):
@@ -378,8 +408,6 @@
     n_norm = float(low_rows * 32 * low_cols * (channels // GROUPS))
     acts2 = acts.reshape(2, 64, 384)
     cot = cotangent.swapaxes(2, 3)
-    w = weights.reshape(12, 3, 9, 2, 96).transpose(3, 0, 1, 2, 4).reshape(2, 12, 3, 864)
-    w = jnp.pad(w, ((0, 0), (0, 4), (0, 0), (0, 32))).reshape(2, 16, 3 * TAPK)
     vm = pl.BlockSpec(memory_space=VMEM)
     dma = pltpu.SemaphoreType.DMA((NCOPY,))
     both = lambda lead, dtype, lanes=LANES: [VMEM((*lead, n), dtype) for n in lanes]
@@ -393,7 +421,7 @@
     dacts, dw = pl.pallas_call(
         lambda *refs: kernel(n_norm, *refs),
         out_shape=(jax.ShapeDtypeStruct((2, 64, 384), BF),
-                   jax.ShapeDtypeStruct((2, 32, 8, 128), F32)),
+                   jax.ShapeDtypeStruct((12, 27, 192), F32)),
         in_specs=[vm] * 5,
         out_specs=(vm, vm),
         scratch_shapes=[
@@ -401,6 +429,7 @@
             VMEM((2, 8, 128), F32), VMEM((2, 15, 8, 128), F32),
             VMEM((TAPK, 768), BF), VMEM((TAPK, 768), BF),
             VMEM((2, 192, 256), BF), VMEM((2, 192, 256), BF),
+            VMEM((16, 3 * TAPK), F32), VMEM((2, 16, 3 * TAPK), F32),
             *both((4, 16), BF), *both((4, 48), BF), *ring(48), *ring(16),
             VMEM((32, 8, 128), F32), VMEM((3, 8, 8, 128), F32), VMEM((8, 8, 128), F32),
             VMEM((2, 32, 8, 128), F32),
@@ -411,13 +440,8 @@
         compiler_params=pltpu.CompilerParams(
             collective_id=0, has_side_effects=True, vmem_limit_bytes=60 * 1024 * 1024),
         name="backward",
-    )(acts2, cot, w, gamma, beta)
-    top = dw[:, :21]
-    rest = dw[:, 21:].reshape(2, 22, 4, 128)[:, :21]
-    flat = jnp.concatenate([top, rest], 2).reshape(2, 3, 7, 12, 128)
-    flat = flat.transpose(3, 1, 0, 2, 4).reshape(12, 3, 2, TAPK)[..., :864]
-    d_weights = flat.reshape(12, 3, 2, 9, 96).transpose(0, 1, 3, 2, 4).reshape(12, 27, 192)
-    return dacts.reshape(2, 1, 64, 384), d_weights
+    )(acts2, cot, weights, gamma, beta)
+    return dacts.reshape(2, 1, 64, 384), dw
 
 
 def solution(mesh):

time: 62.9 us -> 58.8 us (0.935)
  local copies, waits for them, and re-layouts: 6.53 us -> 3.31 us
  Pallas kernels: 55.1 us -> 53.9 us
    reshape x8 -> x0, local copies, waits for them, and re-layouts: 3.73 us -> none  [the longest x3 1.39 us: shards(): weights.reshape(12, 3, 9, 2, 96).transpose(3, 0, 1, 2, 4)]
    unnamed x4 -> x2, local copies, waits for them, and re-layouts: 0.71 us -> 3.31 us
    slice x3 -> x0, local copies, waits for them, and re-layouts: 1.84 us -> none  [the longest x1 0.93 us: shards(): top = dw[:, :21]]
    pallas_call x1, Pallas kernels: 55.1 us -> 53.9 us  [shards(): pl.pallas_call(lambda *refs: kernel(n_norm, *refs), out_shape=(jax.ShapeD...]
where the time goes in v3:
time: 58.8 us; the launch traced here: 57.9 us
  Pallas kernels  53.9 us (92%)
  local copies, waits for them, and re-layouts  3.31 us (6%)
  between operations  0.64 us (1%)
    pallas_call x1, Pallas kernels, shards(): pl.pallas_call(lambda *refs: kernel(n_norm, *refs), out_shape=(jax.ShapeD...  53.9 us
    unnamed x2, local copies, waits for them, and re-layouts  3.31 us

profile of v3, /device:TPU:2, one launch (start us, length us, event | category | flops | bytes accessed | tf_op | source)
XLA Modules:
  0.0 57.9 jit_solution(4273995075648262826)
XLA Ops:
  0.6 53.9 %backward.1 = (bf16[2,64,384]{2,1,0:T(8,128)(2,1)}, f32[12,27,192]{2,1,0:T(8,128)}) custom-call(bf16[2,64,384]{2,1,0:T(8,128)(2,1)} %bitcast.7, bf16[2,2,192,128]{3,2,1,0:T(8,128)(2,1)} %bitcast.5, bf16[12,27,192]{2,1,0:T(8,128)(2,1)} %refs_2_.1, f32[384]{0:T(512)} %refs_3_.1, f32[384]{0:T(512)} %refs_4_.1), custom_call_target="tpu_custom_call" | custom-call | tf_op jit(solution)/shard_map/backward/pallas_call | solution.py:421
  54.6 1.5 %copy.10 = bf16[2,1,64,384]{3,2,1,0:T(8,128)(2,1)} copy(bf16[2,1,64,384]{3,2,1,0:T(8,128)(2,1)} %bitcast.6) | data formatting | bytes 196608
  56.1 1.8 %copy.11 = f32[12,27,192]{2,1,0:T(8,128)} copy(f32[12,27,192]{2,1,0:T(8,128)} %get-tuple-element.11) | data formatting | bytes 497664

commit v4 on v3

--- a/solution.py
+++ b/solution.py
@@ -26,8 +26,8 @@
     return (v * 5462) >> 16
 
 
-def kernel(n_norm, acts, cot, w, gamma, beta, dacts, dw,
-           actbuf, cotbuf, stat_out, stat_in, ghi, glo, hbuf, hswap, wflat, dflat,
+def kernel(n_norm, acts, cot_hbm, w_hbm, gamma_hbm, beta_hbm, dacts, dw,
+           cot, w, gamma, beta, load_sem, actbuf, cotbuf, stat_out, stat_in, ghi, glo, hbuf, hswap, wflat,
            wy0, wy1, wx0, wx1, dp0, dp1, sb0, sb1,
            r10, r11, r20, r21, ra0, ra1, rb0, rb1, sm0, sm1, sn0, sn1,
            ep0, ep1, eb0, eb1, q10, q11, q20, q21, ea0, ea1, ec0, ec1, tm0, tm1, tn0, tn1,
@@ -70,18 +70,26 @@
         c.start()
         return c
 
+    own = pl.ds(1 + 2 * core, 2)
+    mine, theirs, later = pl.ds(2 * u, 2), pl.ds(2 - 2 * u, 2), pl.ds(4, 2)
+    half = pl.ds(pl.multiple_of(96 * u, 32), 96)
+    other_half = pl.ds(pl.multiple_of(96 - 96 * u, 32), 96)
+    loads = [pltpu.make_async_copy(a, b, load_sem.at[k]) for k, (a, b) in enumerate((
+        (acts, actbuf.at[:, core]), (cot_hbm, cot), (w_hbm, w),
+        (cot_hbm.at[:, :, half], cotbuf.at[mine, own]), (gamma_hbm, gamma), (beta_hbm, beta)))]
+    for c in loads:
+        c.start()
+
     barrier = pltpu.get_barrier_semaphore()
     friends = plane + column + [partner, outer]
     for dev in friends:
         pl.semaphore_signal(barrier, inc=1, device_id=dev, device_id_type=MESH)
     pl.semaphore_wait(barrier, len(friends))
 
-    own = pl.ds(1 + 2 * core, 2)
-    mine, theirs, later = pl.ds(2 * u, 2), pl.ds(2 - 2 * u, 2), pl.ds(4, 2)
-    half = pl.ds(pl.multiple_of(96 * u, 32), 96)
-    other_half = pl.ds(pl.multiple_of(96 - 96 * u, 32), 96)
     line, there = 5 * core, 5 * (1 - core)
-    c_act = copy(acts, actbuf.at[:, core], partner)
+    loads[0].wait()
+    c_act = copy(actbuf.at[:, core], actbuf.at[:, core], partner)
+    loads[1].wait()
     edge_row, inner_row = 1 + 3 * core, 2 + core
     nexts, c_twin, c_next = [], [], []
     for r, dst_row in ((core, edge_row), (1 - core, inner_row)):
@@ -116,6 +124,7 @@
         return f1, f2
 
     first = []
+    loads[2].wait()
     wide_w = w[...].astype(F32)
     wide_w = jnp.where(u == 0, wide_w[..., 0:96], wide_w[..., 96:192])
     for a in range(3):
@@ -128,8 +137,8 @@
         wy[h][p] = wflat[:, 1408 * h:1408 * h + LANES[h]].astype(BF)
         first.append(gather_start(wy[h], p, plus, minus))
 
-    actbuf[:, core] = acts[...]
-    cotbuf[mine, own] = cot[:, :, half, :]
+    for c in loads[3:]:
+        c.wait()
     blk = div12(iota((192, 384), 0))
     pick = iota((192, 384), 1) == iota((192, 384), 0) + 12 * blk + 12 * core
     pick_bf = jnp.where(pick, 1.0, 0.0).astype(BF)
@@ -239,8 +248,6 @@
                 ghi[k:k + 96, 128 * f:128 * f + 128] = hi
                 glo[k:k + 96, 128 * f:128 * f + 128] = (v - hi.astype(F32)).astype(BF)
 
-    fourth = [gather_forward(h, wx[h], *places[h][3:], third[h]) for h in range(2)]
-
     def reduce_start(h, part, sbuf, p, plus, minus, r1, r2, a_in, b_in):
         opp, nxt, prv = lax.rem(p + 2, 4), lax.rem(p + 1, 4), lax.rem(p + 3, 4)
         lo, hi = pl.ds(0, CUTS[h]), pl.ds(CUTS[h], LANES[h] - CUTS[h])
@@ -300,6 +307,13 @@
                 dp[h][j, :, l0:l0 + rows] += d[48 * j:48 * j + 48]
         p, plus, minus = rs_places[h][:3]
         started.append(reduce_start(h, dp[h], sb[h], p, plus, minus, *rs_in[h]))
+
+    fourth = [gather_forward(h, wx[h], *places[h][3:], third[h]) for h in range(2)]
+
+    mids = []
+    for h in range(2):
+        p, plus, minus = rs_places[h][:3]
+        mids.append(reduce_mid(h, dp[h], p, plus, minus, *rs_in[h], *rs_mid[h], started[h]))
 
     ag = []
     for h in range(2):
@@ -319,11 +333,6 @@
         actp[v] = ag[0][:, 256 * v:256 * v + 256] + perm_scr[:, 256 * v:256 * v + 256]
     c_grad = copy(actp.at[1 - u], actin, twin)
 
-    mids = []
-    for h in range(2):
-        p, plus, minus = rs_places[h][:3]
-        mids.append(reduce_mid(h, dp[h], p, plus, minus, *rs_in[h], *rs_mid[h], started[h]))
-
     ep, eb = (ep0, ep1), (eb0, eb1)
     rs_in2 = ((q10, q20, ea0, ec0), (q11, q21, ea1, ec1))
     rs_mid2 = ((tm0, tn0), (tm1, tn1))
@@ -336,24 +345,11 @@
             ep[h][j, 0:12] = whole[12 * j:12 * j + 12]
         p2, plus2, minus2 = rs_places[h][3:]
         second_rs.append(reduce_start(h, ep[h], eb[h], p2, plus2, minus2, *rs_in2[h]))
-    c_grad.wait_recv()
-    norm_grad = (actp[u] + actin[...]) * slope
-    tot2 = group_sums(norm_grad, norm_grad * normed)
-    s2 = stats_start(1, tot2)
-
     mids2 = []
     for h in range(2):
         p2, plus2, minus2 = rs_places[h][3:]
         mids2.append(reduce_mid(h, ep[h], p2, plus2, minus2, *rs_in2[h], *rs_mid2[h],
                                 second_rs[h]))
-
-    tot2 = stats_end(1, tot2, s2)
-    mean2 = tot2[0:4] / n_norm
-    d = inv * (norm_grad - wide(mean2[0:2]) - normed * wide(mean2[2:4]))
-    back = lax.dot_general(d.astype(BF), pick_bf, (((0,), (0,)), ((), ())),
-                           preferred_element_type=F32)
-    dsend[...] = back.astype(BF).reshape(2, 2, 64, 384)
-    c_out = copy(dsend.at[:, 1 - core], drecv, partner)
 
     rest = []
     for h in range(2):
@@ -370,8 +366,11 @@
     for m in range(1, 4):
         owner = lax.rem(pair + m, 4)
         zs.append(copy(fin.at[pl.ds(8 * owner, 8)], zin.at[m - 1], column[2 * m - 1]))
-    c_out.wait_recv()
-    dacts[...] = dsend[:, core] + drecv[...]
+    c_grad.wait_recv()
+    norm_grad = (actp[u] + actin[...]) * slope
+    tot2 = group_sums(norm_grad, norm_grad * normed)
+    s2 = stats_start(1, tot2)
+
     total = fin[pl.ds(8 * pair, 8)]
     for m in range(3):
         zs[m].wait_recv()
@@ -379,8 +378,30 @@
     zred[...] = total
     zg = [copy(zred, zout.at[u, pl.ds(8 * pair, 8)], column[k]) for k in range(7)]
     zout[u, pl.ds(8 * pair, 8)] = total
+    tot2 = stats_end(1, tot2, s2)
+    mean2 = tot2[0:4] / n_norm
+    d = inv * (norm_grad - wide(mean2[0:2]) - normed * wide(mean2[2:4]))
+    back = lax.dot_general(d.astype(BF), pick_bf, (((0,), (0,)), ((), ())),
+                           preferred_element_type=F32)
+    dsend[...] = back.astype(BF).reshape(2, 2, 64, 384)
+    c_out = copy(dsend.at[:, 1 - core], drecv, partner)
+
+    c_out.wait_recv()
+    dacts[...] = dsend[:, core] + drecv[...]
     for c in zg:
         c.wait_recv()
+    dw[...] = zout[...]
+    for c in copies:
+        c.wait_send()
+
+    @pl.when(u == 0)
+    def _():
+        for c in nexts:
+            c.wait_send()
+
+
+def finish(dacts_in, zout, dacts, dw, dflat):
+    dacts[...] = dacts_in[...]
     for v in range(2):
         for k in range(21):
             dflat[v, 0:8, 128 * k:128 * k + 128] = zout[v, k]
@@ -394,13 +415,6 @@
             k = a * TAPK + 96 * b
             dw[:, 9 * a + b, 0:96] = dflat[0, 0:12, k:k + 96]
             dw[:, 9 * a + b, 96:192] = dflat[1, 0:12, k:k + 96]
-    for c in copies:
-        c.wait_send()
-
-    @pl.when(u == 0)
-    def _():
-        for c in nexts:
-            c.wait_send()
 
 
 def shards(acts, gamma, beta, weights, cotangent):
@@ -421,15 +435,17 @@
     dacts, dw = pl.pallas_call(
         lambda *refs: kernel(n_norm, *refs),
         out_shape=(jax.ShapeDtypeStruct((2, 64, 384), BF),
-                   jax.ShapeDtypeStruct((12, 27, 192), F32)),
-        in_specs=[vm] * 5,
+                   jax.ShapeDtypeStruct((2, 32, 8, 128), F32)),
+        in_specs=[pl.BlockSpec(memory_space=pl.ANY)] * 5,
         out_specs=(vm, vm),
         scratch_shapes=[
+            VMEM((2, 2, 192, 128), BF), VMEM((12, 27, 192), BF), VMEM((384,), F32),
+            VMEM((384,), F32), pltpu.SemaphoreType.DMA((6,)),
             VMEM((2, 2, 64, 384), BF), VMEM((6, 6, 96, 128), BF),
             VMEM((2, 8, 128), F32), VMEM((2, 15, 8, 128), F32),
             VMEM((TAPK, 768), BF), VMEM((TAPK, 768), BF),
             VMEM((2, 192, 256), BF), VMEM((2, 192, 256), BF),
-            VMEM((16, 3 * TAPK), F32), VMEM((2, 16, 3 * TAPK), F32),
+            VMEM((16, 3 * TAPK), F32),
             *both((4, 16), BF), *both((4, 48), BF), *ring(48), *ring(16),
             VMEM((32, 8, 128), F32), VMEM((3, 8, 8, 128), F32), VMEM((8, 8, 128), F32),
             VMEM((2, 32, 8, 128), F32),
@@ -438,9 +454,19 @@
             dma, dma,
         ],
         compiler_params=pltpu.CompilerParams(
-            collective_id=0, has_side_effects=True, vmem_limit_bytes=60 * 1024 * 1024),
+            collective_id=0, has_side_effects=True, vmem_limit_bytes=20 * 1024 * 1024),
         name="backward",
     )(acts2, cot, weights, gamma, beta)
+    dacts, dw = pl.pallas_call(
+        finish,
+        out_shape=(jax.ShapeDtypeStruct((2, 64, 384), BF),
+                   jax.ShapeDtypeStruct((12, 27, 192), F32)),
+        in_specs=[vm] * 2,
+        out_specs=(vm, vm),
+        scratch_shapes=[VMEM((2, 16, 3 * TAPK), F32)],
+        compiler_params=pltpu.CompilerParams(vmem_limit_bytes=8 * 1024 * 1024),
+        name="finish",
+    )(dacts, dw)
     return dacts.reshape(2, 1, 64, 384), dw
 
 

time: 58.8 us -> 59.3 us (level)
  local copies, waits for them, and re-layouts: 3.31 us -> 4.1 us
    pallas_call x0 -> x1, Pallas kernels: none -> 1.54 us  [shards(): pl.pallas_call(finish, out_shape=(jax.ShapeDtypeStruct((2, 64, 384), BF),...]
    pallas_call x1, Pallas kernels: 53.9 us -> 52.6 us  [shards(): pl.pallas_call(lambda *refs: kernel(n_norm, *refs), out_shape=(jax.ShapeD...]
    unnamed x2 -> x10, local copies, waits for them, and re-layouts: 3.31 us -> 4.1 us
where the time goes in v4:
time: 59.3 us; the launch traced here: 58.9 us
  Pallas kernels  54.2 us (91%)
  local copies, waits for them, and re-layouts  4.1 us (7%)
  between operations  0.65 us (1%)
    pallas_call x1, Pallas kernels, shards(): pl.pallas_call(lambda *refs: kernel(n_norm, *refs), out_shape=(jax.ShapeD...  52.6 us
    unnamed x10, local copies, waits for them, and re-layouts  4.1 us
    pallas_call x1, Pallas kernels, shards(): pl.pallas_call(finish, out_shape=(jax.ShapeDtypeStruct((2, 64, 384), BF),...  1.54 us

profile of v4, /device:TPU:2, one launch (start us, length us, event | category | flops | bytes accessed | tf_op | source)
XLA Modules:
  0.0 58.9 jit_solution(12002602934396367464)
XLA Ops:
  0.6 0.0 copy-start.3
  0.6 0.7 %copy-done.3 = f32[384]{0:T(512)S(1)} copy-done((f32[384]{0:T(512)S(1)}, f32[384]{0:T(512)}, u32[]{:S(2)}) %copy-start.3) | copy-done | bytes 1560
  1.3 0.0 copy-start
  1.3 0.9 %copy-done = bf16[2,2,128,192]{2,3,1,0:T(8,128)(2,1)S(1)} copy-done((bf16[2,2,128,192]{2,3,1,0:T(8,128)(2,1)S(1)}, bf16[2,2,128,192]{2,3,1,0:T(8,128)(2,1)}, u32[]{:S(2)}) %copy-start) | copy-done | bytes 196632
  2.2 0.0 copy-start.1
  2.2 0.9 %copy-done.1 = bf16[12,27,192]{2,1,0:T(8,128)(2,1)S(1)} copy-done((bf16[12,27,192]{2,1,0:T(8,128)(2,1)S(1)}, bf16[12,27,192]{2,1,0:T(8,128)(2,1)}, u32[]{:S(2)}) %copy-start.1) | copy-done | bytes 124440
  3.2 0.0 copy-start.2
  3.2 0.9 %copy-done.2 = bf16[2,1,64,384]{3,2,1,0:T(8,128)(2,1)S(1)} copy-done((bf16[2,1,64,384]{3,2,1,0:T(8,128)(2,1)S(1)}, bf16[2,1,64,384]{3,2,1,0:T(8,128)(2,1)}, u32[]{:S(2)}) %copy-start.2) | copy-done | bytes 98328
  4.1 0.0 copy-start.4
  4.1 0.7 %copy-done.4 = f32[384]{0:T(512)S(1)} copy-done((f32[384]{0:T(512)S(1)}, f32[384]{0:T(512)}, u32[]{:S(2)}) %copy-start.4) | copy-done | bytes 1560
  4.7 52.6 %backward.1 = (bf16[2,64,384]{2,1,0:T(8,128)(2,1)S(1)}, f32[2,32,8,128]{3,2,1,0:T(8,128)S(1)}) custom-call(bf16[2,64,384]{2,1,0:T(8,128)(2,1)S(1)} %bitcast.6, bf16[2,2,192,128]{3,2,1,0:T(8,128)(2,1)S(1)} %bitcast.5, bf16[12,27,192]{2,1,0:T(8,128)(2,1)S(1)} %copy-done.1, f32[384]{0:T(512)S(1)} %copy-done.3, f32[384]{0:T(512)S(1)} %copy-done.4), custom_call_target="tpu_custom_call" | custom-call | tf_op jit(solution)/shard_map/backward/pallas_call | solution.py:435
  57.4 1.5 %finish.1 = (bf16[2,64,384]{2,1,0:T(8,128)(2,1)}, f32[12,27,192]{2,1,0:T(8,128)}) custom-call(bf16[2,64,384]{2,1,0:T(8,128)(2,1)S(1)} %get-tuple-element.6.dacts_in, f32[2,32,8,128]{3,2,1,0:T(8,128)S(1)} %get-tuple-element.7.zout), custom_call_target="tpu_custom_call" | custom-call | tf_op jit(solution)/shard_map/finish/pallas_call | solution.py:460
Async XLA Ops:
  0.6 0.7 %copy-start.3 = (f32[384]{0:T(512)S(1)}, f32[384]{0:T(512)}, u32[]{:S(2)}) copy-start(f32[384]{0:T(512)} %refs_3_.1) | copy-start | bytes 4612
  1.3 0.9 %copy-start = (bf16[2,2,128,192]{2,3,1,0:T(8,128)(2,1)S(1)}, bf16[2,2,128,192]{2,3,1,0:T(8,128)(2,1)}, u32[]{:S(2)}) copy-start(bf16[2,2,128,192]{2,3,1,0:T(8,128)(2,1)} %param.9) | copy-start | bytes 589828
  2.2 0.9 %copy-start.1 = (bf16[12,27,192]{2,1,0:T(8,128)(2,1)S(1)}, bf16[12,27,192]{2,1,0:T(8,128)(2,1)}, u32[]{:S(2)}) copy-start(bf16[12,27,192]{2,1,0:T(8,128)(2,1)} %refs_2_.1) | copy-start | bytes 373252
  3.2 0.9 %copy-start.2 = (bf16[2,1,64,384]{3,2,1,0:T(8,128)(2,1)S(1)}, bf16[2,1,64,384]{3,2,1,0:T(8,128)(2,1)}, u32[]{:S(2)}) copy-start(bf16[2,1,64,384]{3,2,1,0:T(8,128)(2,1)} %param.5) | copy-start | bytes 294916
  4.1 0.7 %copy-start.4 = (f32[384]{0:T(512)S(1)}, f32[384]{0:T(512)}, u32[]{:S(2)}) copy-start(f32[384]{0:T(512)} %refs_4_.1) | copy-start | bytes 4612

commit v5 on v4

--- a/solution.py
+++ b/solution.py
@@ -30,7 +30,7 @@
            cot, w, gamma, beta, load_sem, actbuf, cotbuf, stat_out, stat_in, ghi, glo, hbuf, hswap, wflat,
            wy0, wy1, wx0, wx1, dp0, dp1, sb0, sb1,
            r10, r11, r20, r21, ra0, ra1, rb0, rb1, sm0, sm1, sn0, sn1,
-           ep0, ep1, eb0, eb1, q10, q11, q20, q21, ea0, ea1, ec0, ec1, tm0, tm1, tn0, tn1,
+           ep0, ep1, q10, q11, q20, q21, ea0, ea1, ec0, ec1, tm0, tm1, tn0, tn1,
            fin, zin, zred, zout, actp, actin, perm_scr, dsend, drecv, send_sem, recv_sem):
     z = lax.axis_index("block")
     tile = lax.axis_index("tile")
@@ -209,6 +209,9 @@
     swap_bf = jnp.where(swap, 1.0, 0.0).astype(BF)
     hswap[u] = jnp.dot(swap_bf, hidden, preferred_element_type=F32).astype(BF)
 
+    early.append(pass_edge(theirs, edge1))
+    late.append(pass_row(later, inner_row, partner, inner_row, c_next[1]))
+    late.append(pass_edge(later, edge2))
     third = []
     for h in range(2):
         for f in second[h]:
@@ -218,9 +221,6 @@
         wx[h][p2] = jnp.concatenate(parts, axis=0).astype(BF)
         third.append(gather_start(wx[h], p2, plus2, minus2))
 
-    early.append(pass_edge(theirs, edge1))
-    late.append(pass_row(later, inner_row, partner, inner_row, c_next[1]))
-    late.append(pass_edge(later, edge2))
     for c in early:
         c.wait_recv()
     left = iota((96, 128), 1) < 64
@@ -251,12 +251,15 @@
     def reduce_start(h, part, sbuf, p, plus, minus, r1, r2, a_in, b_in):
         opp, nxt, prv = lax.rem(p + 2, 4), lax.rem(p + 1, 4), lax.rem(p + 3, 4)
         lo, hi = pl.ds(0, CUTS[h]), pl.ds(CUTS[h], LANES[h] - CUTS[h])
-        sbuf[opp] = part[opp].astype(BF)
+        if sbuf is not part:
+            sbuf[opp] = part[opp].astype(BF)
         o1 = copy(sbuf.at[opp, :, lo], r1, plus)
         o2 = copy(sbuf.at[opp, :, hi], r2, minus)
-        sbuf[nxt] = part[nxt].astype(BF)
+        if sbuf is not part:
+            sbuf[nxt] = part[nxt].astype(BF)
         n1 = copy(sbuf.at[nxt, :, hi], a_in.at[:, hi], plus)
-        sbuf[prv] = part[prv].astype(BF)
+        if sbuf is not part:
+            sbuf[prv] = part[prv].astype(BF)
         n2 = copy(sbuf.at[prv, :, lo], b_in.at[:, lo], minus)
         return o1, o2, n1, n2
 
@@ -264,10 +267,10 @@
         nxt, prv = lax.rem(p + 1, 4), lax.rem(p + 3, 4)
         lo, hi = pl.ds(0, CUTS[h]), pl.ds(CUTS[h], LANES[h] - CUTS[h])
         cs[0].wait_recv()
-        s_1[...] = (part[nxt, :, lo] + r1[...].astype(F32)).astype(BF)
+        s_1[...] = (part[nxt, :, lo] + r1[...].astype(F32)).astype(s_1.dtype)
         m1 = copy(s_1, a_in.at[:, lo], plus)
         cs[1].wait_recv()
-        s_2[...] = (part[prv, :, hi] + r2[...].astype(F32)).astype(BF)
+        s_2[...] = (part[prv, :, hi] + r2[...].astype(F32)).astype(s_2.dtype)
         m2 = copy(s_2, b_in.at[:, hi], minus)
         return m1, m2
 
@@ -315,6 +318,17 @@
         p, plus, minus = rs_places[h][:3]
         mids.append(reduce_mid(h, dp[h], p, plus, minus, *rs_in[h], *rs_mid[h], started[h]))
 
+    ep = (ep0, ep1)
+    rs_in2 = ((q10, q20, ea0, ec0), (q11, q21, ea1, ec1))
+    rs_mid2 = ((tm0, tn0), (tm1, tn1))
+    second_rs = []
+    for h in range(2):
+        p = rs_places[h][0]
+        whole = reduce_end(dp[h], p, rs_in[h][2], rs_in[h][3], started[h], mids[h])
+        for j in range(4):
+            ep[h][j] = whole[12 * j:12 * j + 12]
+        p2, plus2, minus2 = rs_places[h][3:]
+        second_rs.append(reduce_start(h, ep[h], ep[h], p2, plus2, minus2, *rs_in2[h]))
     ag = []
     for h in range(2):
         for f in fourth[h]:
@@ -333,18 +347,6 @@
         actp[v] = ag[0][:, 256 * v:256 * v + 256] + perm_scr[:, 256 * v:256 * v + 256]
     c_grad = copy(actp.at[1 - u], actin, twin)
 
-    ep, eb = (ep0, ep1), (eb0, eb1)
-    rs_in2 = ((q10, q20, ea0, ec0), (q11, q21, ea1, ec1))
-    rs_mid2 = ((tm0, tn0), (tm1, tn1))
-    second_rs = []
-    for h in range(2):
-        p = rs_places[h][0]
-        whole = reduce_end(dp[h], p, rs_in[h][2], rs_in[h][3], started[h], mids[h])
-        for j in range(4):
-            ep[h][j, 8:16] = jnp.zeros((8, LANES[h]), F32)
-            ep[h][j, 0:12] = whole[12 * j:12 * j + 12]
-        p2, plus2, minus2 = rs_places[h][3:]
-        second_rs.append(reduce_start(h, ep[h], eb[h], p2, plus2, minus2, *rs_in2[h]))
     mids2 = []
     for h in range(2):
         p2, plus2, minus2 = rs_places[h][3:]
@@ -375,9 +377,10 @@
     for m in range(3):
         zs[m].wait_recv()
         total = total + zin[m]
+    total = total.reshape(4, 16, 128).astype(BF)
     zred[...] = total
-    zg = [copy(zred, zout.at[u, pl.ds(8 * pair, 8)], column[k]) for k in range(7)]
-    zout[u, pl.ds(8 * pair, 8)] = total
+    zg = [copy(zred, zout.at[u, pl.ds(4 * pair, 4)], column[k]) for k in range(7)]
+    zout[u, pl.ds(4 * pair, 4)] = total
     tot2 = stats_end(1, tot2, s2)
     mean2 = tot2[0:4] / n_norm
     d = inv * (norm_grad - wide(mean2[0:2]) - normed * wide(mean2[2:4]))
@@ -403,10 +406,11 @@
 def finish(dacts_in, zout, dacts, dw, dflat):
     dacts[...] = dacts_in[...]
     for v in range(2):
+        tiles = zout[v].astype(F32).reshape(32, 8, 128)
         for k in range(21):
-            dflat[v, 0:8, 128 * k:128 * k + 128] = zout[v, k]
+            dflat[v, 0:8, 128 * k:128 * k + 128] = tiles[k]
         for m in range(11):
-            two = zout[v, 21 + m]
+            two = tiles[21 + m]
             dflat[v, 8:12, 256 * m:256 * m + 128] = two[0:4]
             if m < 10:
                 dflat[v, 8:12, 256 * m + 128:256 * m + 256] = two[4:8]
@@ -427,16 +431,17 @@
     both = lambda lead, dtype, lanes=LANES: [VMEM((*lead, n), dtype) for n in lanes]
     tails = tuple(n - c for n, c in zip(LANES, CUTS))
 
-    def ring(rows):
-        return (both((4, rows), F32) + both((4, rows), BF) + both((rows,), BF, CUTS)
-                + both((rows,), BF, tails) + both((rows,), BF) + both((rows,), BF)
-                + both((rows,), BF, CUTS) + both((rows,), BF, tails))
+    def ring(rows, dtype):
+        first = both((4, rows), F32) + (both((4, rows), BF) if dtype == BF else [])
+        return (first + both((rows,), dtype, CUTS) + both((rows,), dtype, tails)
+                + both((rows,), dtype) + both((rows,), dtype)
+                + both((rows,), dtype, CUTS) + both((rows,), dtype, tails))
 
     dacts, dw = pl.pallas_call(
         lambda *refs: kernel(n_norm, *refs),
         out_shape=(jax.ShapeDtypeStruct((2, 64, 384), BF),
-                   jax.ShapeDtypeStruct((2, 32, 8, 128), F32)),
-        in_specs=[pl.BlockSpec(memory_space=pl.ANY)] * 5,
+                   jax.ShapeDtypeStruct((2, 16, 16, 128), BF)),
+        in_specs=[pl.BlockSpec(memory_space=pltpu.HBM)] * 5,
         out_specs=(vm, vm),
         scratch_shapes=[
             VMEM((2, 2, 192, 128), BF), VMEM((12, 27, 192), BF), VMEM((384,), F32),
@@ -446,9 +451,9 @@
             VMEM((TAPK, 768), BF), VMEM((TAPK, 768), BF),
             VMEM((2, 192, 256), BF), VMEM((2, 192, 256), BF),
             VMEM((16, 3 * TAPK), F32),
-            *both((4, 16), BF), *both((4, 48), BF), *ring(48), *ring(16),
-            VMEM((32, 8, 128), F32), VMEM((3, 8, 8, 128), F32), VMEM((8, 8, 128), F32),
-            VMEM((2, 32, 8, 128), F32),
+            *both((4, 16), BF), *both((4, 48), BF), *ring(48, BF), *ring(12, F32),
+            VMEM((32, 8, 128), F32), VMEM((3, 8, 8, 128), F32), VMEM((4, 16, 128), BF),
+            VMEM((2, 16, 16, 128), BF),
             VMEM((2, 192, 256), F32), VMEM((192, 256), F32), VMEM((192, 512), F32),
             VMEM((2, 2, 64, 384), BF), VMEM((2, 64, 384), BF),
             dma, dma,
@@ -456,7 +461,7 @@
         compiler_params=pltpu.CompilerParams(
             collective_id=0, has_side_effects=True, vmem_limit_bytes=20 * 1024 * 1024),
         name="backward",
-    )(acts2, cot, weights, gamma, beta)
+    )(*(pltpu.with_memory_space_constraint(v, pltpu.HBM) for v in (acts2, cot, weights, gamma, beta)))
     dacts, dw = pl.pallas_call(
         finish,
         out_shape=(jax.ShapeDtypeStruct((2, 64, 384), BF),

time: 59.3 us -> 52.6 us (0.89)
  local copies, waits for them, and re-layouts: 4.1 us -> 0 us
  Pallas kernels: 54.2 us -> 51.6 us
    unnamed x10 -> x0, local copies, waits for them, and re-layouts: 4.1 us -> none
    pallas_call x1, Pallas kernels: 52.6 us -> 50.1 us  [shards(): pl.pallas_call(lambda *refs: kernel(n_norm, *refs), out_shape=(jax.ShapeD...]
where the time goes in v5:
time: 52.6 us; the launch traced here: 52.3 us
  Pallas kernels  51.6 us (98%)
  between operations  0.64 us (1%)
    pallas_call x1, Pallas kernels, shards(): pl.pallas_call(lambda *refs: kernel(n_norm, *refs), out_shape=(jax.ShapeD...  50.1 us
    pallas_call x1, Pallas kernels, shards(): pl.pallas_call(finish, out_shape=(jax.ShapeDtypeStruct((2, 64, 384), BF),...  1.55 us

profile of v5, /device:TPU:2, one launch (start us, length us, event | category | flops | bytes accessed | tf_op | source)
XLA Modules:
  0.0 52.3 jit_solution(1122678330396975360)
XLA Ops:
  0.6 50.1 %backward.1 = (bf16[2,64,384]{2,1,0:T(8,128)(2,1)S(1)}, bf16[2,16,16,128]{3,2,1,0:T(8,128)(2,1)S(1)}) custom-call(bf16[2,64,384]{2,1,0:T(8,128)(2,1)} %bitcast.6, bf16[2,2,192,128]{3,2,1,0:T(8,128)(2,1)} %bitcast.5, bf16[12,27,192]{2,1,0:T(8,128)(2,1)} %refs_2_.1, f32[384]{0:T(512)} %refs_3_.1, f32[384]{0:T(512)} %refs_4_.1), custom_call_target="tpu_custom_call" | custom-call | tf_op jit(solution)/shard_map/backward/pallas_call | solution.py:440
  50.7 1.5 %finish.1 = (bf16[2,64,384]{2,1,0:T(8,128)(2,1)}, f32[12,27,192]{2,1,0:T(8,128)}) custom-call(bf16[2,64,384]{2,1,0:T(8,128)(2,1)S(1)} %get-tuple-element.6.dacts_in, bf16[2,16,16,128]{3,2,1,0:T(8,128)(2,1)S(1)} %get-tuple-element.7.zout), custom_call_target="tpu_custom_call" | custom-call | tf_op jit(solution)/shard_map/finish/pallas_call | solution.py:465

commit v6 on v5

--- a/solution.py
+++ b/solution.py
@@ -11,11 +11,14 @@
 BF = jnp.bfloat16
 F32 = jnp.float32
 VMEM = pltpu.VMEM
-NCOPY = 110
+NCOPY = 144
 TAPK = 896
 LANES = (1408, 1280)
 CUTS = (768, 640)
 SEGMENTS = (((0, 0, 896, 0), (1, 0, 512, 896)), ((1, 512, 384, 0), (2, 0, 896, 384)))
+STREAMS = ((0, 0, 768, 384), (1, 0, 640, 384), (0, 768, 640, 384), (1, 640, 640, 384))
+STREAM_SEGMENTS = (((0, 0, 768, 0),), ((1, 512, 384, 0), (2, 0, 256, 384)),
+                   ((0, 768, 128, 0), (1, 0, 512, 128)), ((2, 256, 640, 0),))
 
 
 def iota(shape, dim):
@@ -28,10 +31,11 @@
 
 def kernel(n_norm, acts, cot_hbm, w_hbm, gamma_hbm, beta_hbm, dacts, dw,
            cot, w, gamma, beta, load_sem, actbuf, cotbuf, stat_out, stat_in, ghi, glo, hbuf, hswap, wflat,
-           wy0, wy1, wx0, wx1, dp0, dp1, sb0, sb1,
-           r10, r11, r20, r21, ra0, ra1, rb0, rb1, sm0, sm1, sn0, sn1,
-           ep0, ep1, q10, q11, q20, q21, ea0, ea1, ec0, ec1, tm0, tm1, tn0, tn1,
-           fin, zin, zred, zout, actp, actin, perm_scr, dsend, drecv, send_sem, recv_sem):
+           wy0, wy1, wx0, wx1, *rest):
+    dps, sbs, r1s, r2s, ras, rbs, m1s, m2s = (rest[4 * k:4 * k + 4] for k in range(8))
+    eps, q1s, q2s, eas, ecs, t1s, t2s = (rest[32 + 4 * k:36 + 4 * k] for k in range(7))
+    (fin_p, fin_q, zin_p, zin_q, zred_p, zred_q, zout_p, zout_q,
+     actp, actin, perm_scr, dsend, drecv, send_sem, recv_sem) = rest[60:]
     z = lax.axis_index("block")
     tile = lax.axis_index("tile")
     core = lax.rem(tile, 2)
@@ -210,8 +214,6 @@
     hswap[u] = jnp.dot(swap_bf, hidden, preferred_element_type=F32).astype(BF)
 
     early.append(pass_edge(theirs, edge1))
-    late.append(pass_row(later, inner_row, partner, inner_row, c_next[1]))
-    late.append(pass_edge(later, edge2))
     third = []
     for h in range(2):
         for f in second[h]:
@@ -221,6 +223,8 @@
         wx[h][p2] = jnp.concatenate(parts, axis=0).astype(BF)
         third.append(gather_start(wx[h], p2, plus2, minus2))
 
+    late.append(pass_row(later, inner_row, partner, inner_row, c_next[1]))
+    late.append(pass_edge(later, edge2))
     for c in early:
         c.wait_recv()
     left = iota((96, 128), 1) < 64
@@ -229,10 +233,8 @@
     summer = jnp.where((shift == 0) | (shift == 1), 1.0, 0.0).astype(BF)
     ghi[864:896] = jnp.zeros((32, 768), BF)
     glo[864:896] = jnp.zeros((32, 768), BF)
-    for f in range(6):
-        if f == 4:
-            for c in late:
-                c.wait_recv()
+
+    def window_sums(f):
         sums = jnp.dot(cotbuf[f].reshape(576, 128), summer, preferred_element_type=F32)
         if f >= 4:
             sums = jnp.where(pair < 3, sums, 0.0)
@@ -248,9 +250,43 @@
                 ghi[k:k + 96, 128 * f:128 * f + 128] = hi
                 glo[k:k + 96, 128 * f:128 * f + 128] = (v - hi.astype(F32)).astype(BF)
 
-    def reduce_start(h, part, sbuf, p, plus, minus, r1, r2, a_in, b_in):
+    hid = (hbuf, hswap)
+
+    def partial(n, v, first):
+        for a, k0, rows, l0 in STREAM_SEGMENTS[n]:
+            lanes = pl.ds(pl.multiple_of(256 * v + (2 - a) * 128, 128), 256)
+            acc = None
+            for g in (ghi, glo):
+                d = lax.dot_general(hid[STREAMS[n][0]][v], g[k0:k0 + rows, lanes],
+                                    (((1,), (1,)), ((), ())), preferred_element_type=F32)
+                acc = d if acc is None else acc + d
+            for j in range(4):
+                if first:
+                    dps[n][j, :, l0:l0 + rows] = acc[48 * j:48 * j + 48]
+                else:
+                    dps[n][j, :, l0:l0 + rows] += acc[48 * j:48 * j + 48]
+
+    for f in range(4):
+        window_sums(f)
+
+    @pl.when(u == 0)
+    def _():
+        for n in range(4):
+            partial(n, 0, True)
+
+    for c in late:
+        c.wait_recv()
+    for f in range(4, 6):
+        window_sums(f)
+
+    @pl.when(u == 1)
+    def _():
+        for n in range(4):
+            partial(n, 1, True)
+
+    def reduce_start(n, part, sbuf, p, plus, minus, r1, r2, a_in, b_in):
         opp, nxt, prv = lax.rem(p + 2, 4), lax.rem(p + 1, 4), lax.rem(p + 3, 4)
-        lo, hi = pl.ds(0, CUTS[h]), pl.ds(CUTS[h], LANES[h] - CUTS[h])
+        lo, hi = pl.ds(0, STREAMS[n][3]), pl.ds(STREAMS[n][3], STREAMS[n][2] - STREAMS[n][3])
         if sbuf is not part:
             sbuf[opp] = part[opp].astype(BF)
         o1 = copy(sbuf.at[opp, :, lo], r1, plus)
@@ -263,9 +299,9 @@
         n2 = copy(sbuf.at[prv, :, lo], b_in.at[:, lo], minus)
         return o1, o2, n1, n2
 
-    def reduce_mid(h, part, p, plus, minus, r1, r2, a_in, b_in, s_1, s_2, cs):
+    def reduce_mid(n, part, p, plus, minus, r1, r2, a_in, b_in, s_1, s_2, cs):
         nxt, prv = lax.rem(p + 1, 4), lax.rem(p + 3, 4)
-        lo, hi = pl.ds(0, CUTS[h]), pl.ds(CUTS[h], LANES[h] - CUTS[h])
+        lo, hi = pl.ds(0, STREAMS[n][3]), pl.ds(STREAMS[n][3], STREAMS[n][2] - STREAMS[n][3])
         cs[0].wait_recv()
         s_1[...] = (part[nxt, :, lo] + r1[...].astype(F32)).astype(s_1.dtype)
         m1 = copy(s_1, a_in.at[:, lo], plus)
@@ -280,55 +316,78 @@
         return part[p] + a_in[...].astype(F32) + b_in[...].astype(F32)
 
     rs_places = (places[1], places[0])
-    hid = (hbuf, hswap)
-    dp, sb = (dp0, dp1), (sb0, sb1)
-    rs_in = ((r10, r20, ra0, rb0), (r11, r21, ra1, rb1))
-    rs_mid = ((sm0, sn0), (sm1, sn1))
-
-    def partial(h, v):
-        outs = []
-        for a, k0, rows, _ in SEGMENTS[h]:
-            lanes = pl.ds(pl.multiple_of(256 * v + (2 - a) * 128, 128), 256)
-            acc = None
-            for g in (ghi, glo):
-                d = lax.dot_general(hid[h][v], g[k0:k0 + rows, lanes], (((1,), (1,)), ((), ())),
-                                    preferred_element_type=F32)
-                acc = d if acc is None else acc + d
-            outs.append(acc)
-        return outs
-
-    for h in range(2):
-        for (a, k0, rows, l0), d in zip(SEGMENTS[h], partial(h, u)):
-            for j in range(4):
-                dp[h][j, :, l0:l0 + rows] = d[48 * j:48 * j + 48]
+    started, mids, started2, mids2 = [None] * 4, [None] * 4, [None] * 4, [None] * 4
+
+    def first_start(n):
+        p, plus, minus = rs_places[STREAMS[n][0]][:3]
+        started[n] = reduce_start(n, dps[n], sbs[n], p, plus, minus,
+                                  r1s[n], r2s[n], ras[n], rbs[n])
+
+    def first_mid(n):
+        p, plus, minus = rs_places[STREAMS[n][0]][:3]
+        mids[n] = reduce_mid(n, dps[n], p, plus, minus, r1s[n], r2s[n], ras[n], rbs[n],
+                             m1s[n], m2s[n], started[n])
+
+    def second_start(n):
+        p, _, _, p2, plus2, minus2 = rs_places[STREAMS[n][0]]
+        whole = reduce_end(dps[n], p, ras[n], rbs[n], started[n], mids[n])
+        for j in range(4):
+            eps[n][j] = whole[12 * j:12 * j + 12]
+        started2[n] = reduce_start(n, eps[n], eps[n], p2, plus2, minus2,
+                                   q1s[n], q2s[n], eas[n], ecs[n])
+
+    def second_mid(n):
+        p2, plus2, minus2 = rs_places[STREAMS[n][0]][3:]
+        mids2[n] = reduce_mid(n, eps[n], p2, plus2, minus2, q1s[n], q2s[n], eas[n], ecs[n],
+                              t1s[n], t2s[n], started2[n])
+
+    def pack(fin, streams):
+        tops, rests = [], []
+        for n in streams:
+            p2 = rs_places[STREAMS[n][0]][3]
+            done = reduce_end(eps[n], p2, eas[n], ecs[n], started2[n], mids2[n])
+            for k in range(STREAMS[n][2] // 128):
+                tops.append(done[0:8, 128 * k:128 * k + 128])
+                rests.append(done[8:12, 128 * k:128 * k + 128])
+        if len(rests) % 2:
+            rests.append(jnp.zeros((4, 128), F32))
+        tops += [jnp.concatenate(rests[2 * m:2 * m + 2], axis=0) for m in range(len(rests) // 2)]
+        while len(tops) < fin.shape[0]:
+            tops.append(jnp.zeros((8, 128), F32))
+        for k, v in enumerate(tops):
+            fin[k] = v
+
+    def z_start(fin, zin):
+        size = fin.shape[0] // 4
+        return [copy(fin.at[pl.ds(size * lax.rem(pair + m, 4), size)], zin.at[m - 1],
+                     column[2 * m - 1]) for m in range(1, 4)]
+
+    def z_gather(fin, zin, zred, zout, cs):
+        size = fin.shape[0] // 4
+        total = fin[pl.ds(size * pair, size)]
+        for m in range(3):
+            cs[m].wait_recv()
+            total = total + zin[m]
+        total = total.reshape(size // 2, 16, 128).astype(BF)
+        zred[...] = total
+        place = pl.ds(size // 2 * pair, size // 2)
+        gs = [copy(zred, zout.at[u, place], column[k]) for k in range(7)]
+        zout[u, place] = total
+        return gs
+
     c_hid.wait_recv()
     hswap[1 - u] = jnp.dot(swap_bf, hbuf[1 - u], preferred_element_type=F32).astype(BF)
-    started = []
-    for h in range(2):
-        for (a, k0, rows, l0), d in zip(SEGMENTS[h], partial(h, 1 - u)):
-            for j in range(4):
-                dp[h][j, :, l0:l0 + rows] += d[48 * j:48 * j + 48]
-        p, plus, minus = rs_places[h][:3]
-        started.append(reduce_start(h, dp[h], sb[h], p, plus, minus, *rs_in[h]))
+    for n in range(4):
+        partial(n, 1 - u, False)
+        first_start(n)
 
     fourth = [gather_forward(h, wx[h], *places[h][3:], third[h]) for h in range(2)]
 
-    mids = []
-    for h in range(2):
-        p, plus, minus = rs_places[h][:3]
-        mids.append(reduce_mid(h, dp[h], p, plus, minus, *rs_in[h], *rs_mid[h], started[h]))
-
-    ep = (ep0, ep1)
-    rs_in2 = ((q10, q20, ea0, ec0), (q11, q21, ea1, ec1))
-    rs_mid2 = ((tm0, tn0), (tm1, tn1))
-    second_rs = []
-    for h in range(2):
-        p = rs_places[h][0]
-        whole = reduce_end(dp[h], p, rs_in[h][2], rs_in[h][3], started[h], mids[h])
-        for j in range(4):
-            ep[h][j] = whole[12 * j:12 * j + 12]
-        p2, plus2, minus2 = rs_places[h][3:]
-        second_rs.append(reduce_start(h, ep[h], ep[h], p2, plus2, minus2, *rs_in2[h]))
+    for n in range(4):
+        first_mid(n)
+    for n in range(4):
+        second_start(n)
+
     ag = []
     for h in range(2):
         for f in fourth[h]:
@@ -347,40 +406,22 @@
         actp[v] = ag[0][:, 256 * v:256 * v + 256] + perm_scr[:, 256 * v:256 * v + 256]
     c_grad = copy(actp.at[1 - u], actin, twin)
 
-    mids2 = []
-    for h in range(2):
-        p2, plus2, minus2 = rs_places[h][3:]
-        mids2.append(reduce_mid(h, ep[h], p2, plus2, minus2, *rs_in2[h], *rs_mid2[h],
-                                second_rs[h]))
-
-    rest = []
-    for h in range(2):
-        p2 = rs_places[h][3]
-        done = reduce_end(ep[h], p2, rs_in2[h][2], rs_in2[h][3], second_rs[h], mids2[h])
-        for k in range(LANES[h] // 128):
-            fin[11 * h + k] = done[0:8, 128 * k:128 * k + 128]
-            rest.append(done[8:12, 128 * k:128 * k + 128])
-    rest.append(jnp.zeros((4, 128), F32))
-    for m in range(11):
-        fin[21 + m] = jnp.concatenate([rest[2 * m], rest[2 * m + 1]], axis=0)
-
-    zs = []
-    for m in range(1, 4):
-        owner = lax.rem(pair + m, 4)
-        zs.append(copy(fin.at[pl.ds(8 * owner, 8)], zin.at[m - 1], column[2 * m - 1]))
+    for n in range(2):
+        second_mid(n)
+    for n in range(2, 4):
+        second_mid(n)
+    pack(fin_p, (0, 1))
+    zs_p = z_start(fin_p, zin_p)
+    pack(fin_q, (2, 3))
+    zs_q = z_start(fin_q, zin_q)
+
     c_grad.wait_recv()
     norm_grad = (actp[u] + actin[...]) * slope
     tot2 = group_sums(norm_grad, norm_grad * normed)
     s2 = stats_start(1, tot2)
 
-    total = fin[pl.ds(8 * pair, 8)]
-    for m in range(3):
-        zs[m].wait_recv()
-        total = total + zin[m]
-    total = total.reshape(4, 16, 128).astype(BF)
-    zred[...] = total
-    zg = [copy(zred, zout.at[u, pl.ds(4 * pair, 4)], column[k]) for k in range(7)]
-    zout[u, pl.ds(4 * pair, 4)] = total
+    zg = z_gather(fin_p, zin_p, zred_p, zout_p, zs_p)
+    zg += z_gather(fin_q, zin_q, zred_q, zout_q, zs_q)
     tot2 = stats_end(1, tot2, s2)
     mean2 = tot2[0:4] / n_norm
     d = inv * (norm_grad - wide(mean2[0:2]) - normed * wide(mean2[2:4]))
@@ -393,7 +434,8 @@
     dacts[...] = dsend[:, core] + drecv[...]
     for c in zg:
         c.wait_recv()
-    dw[...] = zout[...]
+    dw[:, 0:12] = zout_p[...]
+    dw[:, 12:20] = zout_q[...]
     for c in copies:
         c.wait_send()
 
@@ -406,14 +448,13 @@
 def finish(dacts_in, zout, dacts, dw, dflat):
     dacts[...] = dacts_in[...]
     for v in range(2):
-        tiles = zout[v].astype(F32).reshape(32, 8, 128)
-        for k in range(21):
-            dflat[v, 0:8, 128 * k:128 * k + 128] = tiles[k]
-        for m in range(11):
-            two = tiles[21 + m]
-            dflat[v, 8:12, 256 * m:256 * m + 128] = two[0:4]
-            if m < 10:
-                dflat[v, 8:12, 256 * m + 128:256 * m + 256] = two[4:8]
+        tiles = zout[v].astype(F32).reshape(40, 8, 128)
+        for first, places in ((0, (0, 1, 2, 3, 4, 5, 11, 12, 13, 14, 15)),
+                              (24, (6, 7, 8, 9, 10, 16, 17, 18, 19, 20))):
+            for m, k in enumerate(places):
+                dflat[v, 0:8, 128 * k:128 * k + 128] = tiles[first + m]
+                two = tiles[first + len(places) + m // 2]
+                dflat[v, 8:12, 128 * k:128 * k + 128] = two[4 * (m % 2):4 * (m % 2) + 4]
     for a in range(3):
         for b in range(9):
             k = a * TAPK + 96 * b
@@ -429,18 +470,21 @@
     vm = pl.BlockSpec(memory_space=VMEM)
     dma = pltpu.SemaphoreType.DMA((NCOPY,))
     both = lambda lead, dtype, lanes=LANES: [VMEM((*lead, n), dtype) for n in lanes]
-    tails = tuple(n - c for n, c in zip(LANES, CUTS))
+
+    sizes = tuple(v[2] for v in STREAMS)
+    cuts = tuple(v[3] for v in STREAMS)
+    tails = tuple(n - c for n, c in zip(sizes, cuts))
 
     def ring(rows, dtype):
-        first = both((4, rows), F32) + (both((4, rows), BF) if dtype == BF else [])
-        return (first + both((rows,), dtype, CUTS) + both((rows,), dtype, tails)
-                + both((rows,), dtype) + both((rows,), dtype)
-                + both((rows,), dtype, CUTS) + both((rows,), dtype, tails))
+        first = both((4, rows), F32, sizes) + (both((4, rows), BF, sizes) if dtype == BF else [])
+        return (first + both((rows,), dtype, cuts) + both((rows,), dtype, tails)
+                + both((rows,), dtype, sizes) + both((rows,), dtype, sizes)
+                + both((rows,), dtype, cuts) + both((rows,), dtype, tails))
 
     dacts, dw = pl.pallas_call(
         lambda *refs: kernel(n_norm, *refs),
         out_shape=(jax.ShapeDtypeStruct((2, 64, 384), BF),
-                   jax.ShapeDtypeStruct((2, 16, 16, 128), BF)),
+                   jax.ShapeDtypeStruct((2, 20, 16, 128), BF)),
         in_specs=[pl.BlockSpec(memory_space=pltpu.HBM)] * 5,
         out_specs=(vm, vm),
         scratch_shapes=[
@@ -452,8 +496,10 @@
             VMEM((2, 192, 256), BF), VMEM((2, 192, 256), BF),
             VMEM((16, 3 * TAPK), F32),
             *both((4, 16), BF), *both((4, 48), BF), *ring(48, BF), *ring(12, F32),
-            VMEM((32, 8, 128), F32), VMEM((3, 8, 8, 128), F32), VMEM((4, 16, 128), BF),
-            VMEM((2, 16, 16, 128), BF),
+            VMEM((24, 8, 128), F32), VMEM((16, 8, 128), F32),
+            VMEM((3, 6, 8, 128), F32), VMEM((3, 4, 8, 128), F32),
+            VMEM((3, 16, 128), BF), VMEM((2, 16, 128), BF),
+            VMEM((2, 12, 16, 128), BF), VMEM((2, 8, 16, 128), BF),
             VMEM((2, 192, 256), F32), VMEM((192, 256), F32), VMEM((192, 512), F32),
             VMEM((2, 2, 64, 384), BF), VMEM((2, 64, 384), BF),
             dma, dma,

time: 52.6 us -> 52.9 us (level)
  Pallas kernels: 51.6 us -> 52.2 us
    pallas_call x1, Pallas kernels: 50.1 us -> 50.6 us  [shards(): pl.pallas_call(lambda *refs: kernel(n_norm, *refs), out_shape=(jax.ShapeD...]
where the time goes in v6:
time: 52.9 us; the launch traced here: 52.8 us
  Pallas kernels  52.2 us (99%)
  between operations  0.64 us (1%)
    pallas_call x1, Pallas kernels, shards(): pl.pallas_call(lambda *refs: kernel(n_norm, *refs), out_shape=(jax.ShapeD...  50.6 us
    pallas_call x1, Pallas kernels, shards(): pl.pallas_call(finish, out_shape=(jax.ShapeDtypeStruct((2, 64, 384), BF),...  1.54 us

profile of v6, /device:TPU:2, one launch (start us, length us, event | category | flops | bytes accessed | tf_op | source)
XLA Modules:
  0.0 52.8 jit_solution(9604214317687708086)
XLA Ops:
  0.6 50.6 %backward.1 = (bf16[2,64,384]{2,1,0:T(8,128)(2,1)S(1)}, bf16[2,20,16,128]{3,2,1,0:T(8,128)(2,1)S(1)}) custom-call(bf16[2,64,384]{2,1,0:T(8,128)(2,1)} %bitcast.6, bf16[2,2,192,128]{3,2,1,0:T(8,128)(2,1)} %bitcast.5, bf16[12,27,192]{2,1,0:T(8,128)(2,1)} %refs_2_.1, f32[384]{0:T(512)} %refs_3_.1, f32[384]{0:T(512)} %refs_4_.1), custom_call_target="tpu_custom_call" | custom-call | tf_op jit(solution)/shard_map/backward/pallas_call | solution.py:484
  51.3 1.5 %finish.1 = (bf16[2,64,384]{2,1,0:T(8,128)(2,1)}, f32[12,27,192]{2,1,0:T(8,128)}) custom-call(bf16[2,64,384]{2,1,0:T(8,128)(2,1)S(1)} %get-tuple-element.6.dacts_in, bf16[2,20,16,128]{3,2,1,0:T(8,128)(2,1)S(1)} %get-tuple-element.7.zout), custom_call_target="tpu_custom_call" | custom-call | tf_op jit(solution)/shard_map/finish/pallas_call | solution.py:511

commit v7 on v6

--- a/solution.py
+++ b/solution.py
@@ -16,6 +16,7 @@
 LANES = (1408, 1280)
 CUTS = (768, 640)
 SEGMENTS = (((0, 0, 896, 0), (1, 0, 512, 896)), ((1, 512, 384, 0), (2, 0, 896, 384)))
+NARROW = (1, 2)
 STREAMS = ((0, 0, 768, 384), (1, 0, 640, 384), (0, 768, 640, 384), (1, 640, 640, 384))
 STREAM_SEGMENTS = (((0, 0, 768, 0),), ((1, 512, 384, 0), (2, 0, 256, 384)),
                    ((0, 768, 128, 0), (1, 0, 512, 128)), ((2, 256, 640, 0),))
@@ -34,7 +35,7 @@
            wy0, wy1, wx0, wx1, *rest):
     dps, sbs, r1s, r2s, ras, rbs, m1s, m2s = (rest[4 * k:4 * k + 4] for k in range(8))
     eps, q1s, q2s, eas, ecs, t1s, t2s = (rest[32 + 4 * k:36 + 4 * k] for k in range(7))
-    (fin_p, fin_q, zin_p, zin_q, zred_p, zred_q, zout_p, zout_q,
+    (fin_p, fin_q, zin_p, zin_q, zsend_p, zsend_q, znarrow_p, znarrow_q, zred_p, zred_q, zout_p, zout_q,
      actp, actin, perm_scr, dsend, drecv, send_sem, recv_sem) = rest[60:]
     z = lax.axis_index("block")
     tile = lax.axis_index("tile")
@@ -88,12 +89,30 @@
     friends = plane + column + [partner, outer]
     for dev in friends:
         pl.semaphore_signal(barrier, inc=1, device_id=dev, device_id_type=MESH)
+    places = ((y, yp, ym, x, xp, xm), (x, xp, xm, y, yp, ym))
+
+    loads[2].wait()
+    wide_w = w[...].astype(F32)
+    wide_w = jnp.where(u == 0, wide_w[..., 0:96], wide_w[..., 96:192])
+    for a in range(3):
+        for b in range(9):
+            k = a * TAPK + 96 * b
+            wflat[0:12, k:k + 96] = wide_w[:, 9 * a + b, :]
+        wflat[0:12, a * TAPK + 864:a * TAPK + TAPK] = jnp.zeros((12, 32), F32)
+    for h in range(2):
+        wy[h][places[h][0]] = wflat[:, 1408 * h:1408 * h + LANES[h]].astype(BF)
+    for c in loads[3:] + loads[0:2]:
+        c.wait()
+    blk = div12(iota((192, 384), 0))
+    pick = iota((192, 384), 1) == iota((192, 384), 0) + 12 * blk + 12 * core
+    pick_bf = jnp.where(pick, 1.0, 0.0).astype(BF)
+    gcol = jnp.sum(jnp.where(pick, gamma[...][None, :], 0.0), axis=1, keepdims=True)
+    bcol = jnp.sum(jnp.where(pick, beta[...][None, :], 0.0), axis=1, keepdims=True)
+    member = [iota((192, 128), 1) == div12(iota((192, 128), 0)) + 16 * k for k in range(4)]
     pl.semaphore_wait(barrier, len(friends))
 
     line, there = 5 * core, 5 * (1 - core)
-    loads[0].wait()
     c_act = copy(actbuf.at[:, core], actbuf.at[:, core], partner)
-    loads[1].wait()
     edge_row, inner_row = 1 + 3 * core, 2 + core
     nexts, c_twin, c_next = [], [], []
     for r, dst_row in ((core, edge_row), (1 - core, inner_row)):
@@ -111,8 +130,6 @@
 
     c_pair = copy(cot.at[:, :, half], cotbuf.at[mine, own], partner)
     c_edge = copy(cot.at[:, core, half], cotbuf.at[mine, there], outer)
-
-    places = ((y, yp, ym, x, xp, xm), (x, xp, xm, y, yp, ym))
 
     def gather_start(buf, p, plus, minus):
         return copy(buf.at[p], buf.at[p], plus), copy(buf.at[p], buf.at[p], minus)
@@ -128,41 +145,26 @@
         return f1, f2
 
     first = []
-    loads[2].wait()
-    wide_w = w[...].astype(F32)
-    wide_w = jnp.where(u == 0, wide_w[..., 0:96], wide_w[..., 96:192])
-    for a in range(3):
-        for b in range(9):
-            k = a * TAPK + 96 * b
-            wflat[0:12, k:k + 96] = wide_w[:, 9 * a + b, :]
-        wflat[0:12, a * TAPK + 864:a * TAPK + TAPK] = jnp.zeros((12, 32), F32)
     for h in range(2):
         p, plus, minus = places[h][:3]
-        wy[h][p] = wflat[:, 1408 * h:1408 * h + LANES[h]].astype(BF)
         first.append(gather_start(wy[h], p, plus, minus))
 
-    for c in loads[3:]:
-        c.wait()
-    blk = div12(iota((192, 384), 0))
-    pick = iota((192, 384), 1) == iota((192, 384), 0) + 12 * blk + 12 * core
-    pick_bf = jnp.where(pick, 1.0, 0.0).astype(BF)
-    gcol = jnp.sum(jnp.where(pick, gamma[...][None, :], 0.0), axis=1, keepdims=True)
-    bcol = jnp.sum(jnp.where(pick, beta[...][None, :], 0.0), axis=1, keepdims=True)
-    member = iota((192, 128), 1) == div12(iota((192, 128), 0))
     c_act.wait_recv()
     xt = lax.dot_general(pick_bf, actbuf[...].reshape(256, 384), (((1,), (1,)), ((), ())),
                          preferred_element_type=F32)
 
     def group_sums(a, b):
-        lines = []
-        for value in (a, b):
-            for t in range(2):
-                c = jnp.sum(value[:, 128 * t:128 * t + 128], axis=1, keepdims=True)
-                lines.append(jnp.sum(jnp.where(member, c, 0.0), axis=0, keepdims=True))
-        return jnp.concatenate(lines + [jnp.zeros((4, 128), F32)], axis=0)
-
-    def spread(v):
-        return jnp.sum(jnp.where(member, v, 0.0), axis=1, keepdims=True)
+        total = jnp.zeros((192, 128), F32)
+        for k in range(4):
+            value = (a, b)[k // 2][:, 128 * (k % 2):128 * (k % 2) + 128]
+            total = total + jnp.where(member[k], jnp.sum(value, axis=1, keepdims=True), 0.0)
+        return jnp.sum(total, axis=0, keepdims=True)
+
+    def spread(v, k):
+        return jnp.sum(jnp.where(member[k], v, 0.0), axis=1, keepdims=True)
+
+    def wide(first, second):
+        return jnp.concatenate([jnp.broadcast_to(v, (192, 128)) for v in (first, second)], axis=1)
 
     def stats_start(k, total):
         stat_out[k] = total
@@ -187,8 +189,8 @@
         return copy(cotbuf.at[frames, r], cotbuf.at[frames, to], device)
 
     early, late = [c_pair], []
+    early.append(pass_edge(mine, c_edge))
     second = [gather_forward(h, wy[h], *places[h][:3], first[h]) for h in range(2)]
-    early.append(pass_edge(mine, c_edge))
     edge1 = pass_row(theirs, edge_row, outer, there, c_twin[0])
     early.append(pass_row(theirs, edge_row, partner, edge_row, None))
     edge2 = pass_row(later, edge_row, outer, there, c_next[0])
@@ -196,12 +198,9 @@
     early.append(pass_row(theirs, inner_row, partner, inner_row, c_twin[1]))
 
     tot1 = stats_end(0, tot1, s1)
-    mean_l = tot1[0:2] / n_norm
-    inv_l = lax.rsqrt(tot1[2:4] / n_norm - mean_l * mean_l + NORM_EPS)
-    wide = lambda m: jnp.concatenate(
-        [jnp.broadcast_to(spread(m[t:t + 1]), (192, 128)) for t in range(2)], axis=1)
-    inv = wide(inv_l)
-    normed = (xt - wide(mean_l)) * inv
+    stats = [spread(tot1, k) / n_norm for k in range(4)]
+    inv = wide(*(lax.rsqrt(stats[2 + t] - stats[t] * stats[t] + NORM_EPS) for t in range(2)))
+    normed = (xt - wide(*stats[0:2])) * inv
     shifted = normed * gcol + bcol
     gate = jax.nn.sigmoid(shifted)
     hidden = (shifted * gate).astype(BF)
@@ -357,21 +356,31 @@
         for k, v in enumerate(tops):
             fin[k] = v
 
-    def z_start(fin, zin):
+    def z_start(fin, zin, zsend, znarrow):
         size = fin.shape[0] // 4
-        return [copy(fin.at[pl.ds(size * lax.rem(pair + m, 4), size)], zin.at[m - 1],
-                     column[2 * m - 1]) for m in range(1, 4)]
-
-    def z_gather(fin, zin, zred, zout, cs):
+        cs = []
+        for m in (2, 1, 3):
+            place = pl.ds(size * lax.rem(pair + m, 4), size)
+            if m in NARROW:
+                zsend[m - 1] = fin[place].astype(BF)
+                cs.append(copy(zsend.at[m - 1], znarrow.at[m - 1], column[2 * m - 1]))
+            else:
+                cs.append(copy(fin.at[place], zin.at[m - 1], column[2 * m - 1]))
+        return cs
+
+    def z_gather(fin, zin, znarrow, zred, zout, cs):
         size = fin.shape[0] // 4
         total = fin[pl.ds(size * pair, size)]
-        for m in range(3):
-            cs[m].wait_recv()
-            total = total + zin[m]
-        total = total.reshape(size // 2, 16, 128).astype(BF)
+        for m, c in zip((2, 1, 3), cs):
+            c.wait_recv()
+            if m in NARROW:
+                total = total + znarrow[m - 1].astype(F32)
+            else:
+                total = total + zin[m - 1]
+        total = total.astype(BF)
         zred[...] = total
-        place = pl.ds(size // 2 * pair, size // 2)
-        gs = [copy(zred, zout.at[u, place], column[k]) for k in range(7)]
+        place = pl.ds(size * pair, size)
+        gs = [copy(zred, zout.at[u, place], column[k]) for k in (3, 2, 4, 1, 5, 0, 6)]
         zout[u, place] = total
         return gs
 
@@ -411,20 +420,20 @@
     for n in range(2, 4):
         second_mid(n)
     pack(fin_p, (0, 1))
-    zs_p = z_start(fin_p, zin_p)
+    zs_p = z_start(fin_p, zin_p, zsend_p, znarrow_p)
     pack(fin_q, (2, 3))
-    zs_q = z_start(fin_q, zin_q)
+    zs_q = z_start(fin_q, zin_q, zsend_q, znarrow_q)
 
     c_grad.wait_recv()
     norm_grad = (actp[u] + actin[...]) * slope
     tot2 = group_sums(norm_grad, norm_grad * normed)
     s2 = stats_start(1, tot2)
 
-    zg = z_gather(fin_p, zin_p, zred_p, zout_p, zs_p)
-    zg += z_gather(fin_q, zin_q, zred_q, zout_q, zs_q)
+    zg = z_gather(fin_p, zin_p, znarrow_p, zred_p, zout_p, zs_p)
+    zg += z_gather(fin_q, zin_q, znarrow_q, zred_q, zout_q, zs_q)
     tot2 = stats_end(1, tot2, s2)
-    mean2 = tot2[0:4] / n_norm
-    d = inv * (norm_grad - wide(mean2[0:2]) - normed * wide(mean2[2:4]))
+    mean2 = [spread(tot2, k) / n_norm for k in range(4)]
+    d = inv * (norm_grad - wide(*mean2[0:2]) - normed * wide(*mean2[2:4]))
     back = lax.dot_general(d.astype(BF), pick_bf, (((0,), (0,)), ((), ())),
                            preferred_element_type=F32)
     dsend[...] = back.astype(BF).reshape(2, 2, 64, 384)
@@ -434,8 +443,8 @@
     dacts[...] = dsend[:, core] + drecv[...]
     for c in zg:
         c.wait_recv()
-    dw[:, 0:12] = zout_p[...]
-    dw[:, 12:20] = zout_q[...]
+    dw[:, 0:20] = zout_p[...]
+    dw[:, 20:36] = zout_q[...]
     for c in copies:
         c.wait_send()
 
@@ -448,9 +457,9 @@
 def finish(dacts_in, zout, dacts, dw, dflat):
     dacts[...] = dacts_in[...]
     for v in range(2):
-        tiles = zout[v].astype(F32).reshape(40, 8, 128)
+        tiles = zout[v].astype(F32)
         for first, places in ((0, (0, 1, 2, 3, 4, 5, 11, 12, 13, 14, 15)),
-                              (24, (6, 7, 8, 9, 10, 16, 17, 18, 19, 20))):
+                              (20, (6, 7, 8, 9, 10, 16, 17, 18, 19, 20))):
             for m, k in enumerate(places):
                 dflat[v, 0:8, 128 * k:128 * k + 128] = tiles[first + m]
                 two = tiles[first + len(places) + m // 2]
@@ -484,22 +493,24 @@
     dacts, dw = pl.pallas_call(
         lambda *refs: kernel(n_norm, *refs),
         out_shape=(jax.ShapeDtypeStruct((2, 64, 384), BF),
-                   jax.ShapeDtypeStruct((2, 20, 16, 128), BF)),
+                   jax.ShapeDtypeStruct((2, 36, 8, 128), BF)),
         in_specs=[pl.BlockSpec(memory_space=pltpu.HBM)] * 5,
         out_specs=(vm, vm),
         scratch_shapes=[
             VMEM((2, 2, 192, 128), BF), VMEM((12, 27, 192), BF), VMEM((384,), F32),
             VMEM((384,), F32), pltpu.SemaphoreType.DMA((6,)),
             VMEM((2, 2, 64, 384), BF), VMEM((6, 6, 96, 128), BF),
-            VMEM((2, 8, 128), F32), VMEM((2, 15, 8, 128), F32),
+            VMEM((2, 1, 128), F32), VMEM((2, 15, 1, 128), F32),
             VMEM((TAPK, 768), BF), VMEM((TAPK, 768), BF),
             VMEM((2, 192, 256), BF), VMEM((2, 192, 256), BF),
             VMEM((16, 3 * TAPK), F32),
             *both((4, 16), BF), *both((4, 48), BF), *ring(48, BF), *ring(12, F32),
-            VMEM((24, 8, 128), F32), VMEM((16, 8, 128), F32),
-            VMEM((3, 6, 8, 128), F32), VMEM((3, 4, 8, 128), F32),
-            VMEM((3, 16, 128), BF), VMEM((2, 16, 128), BF),
-            VMEM((2, 12, 16, 128), BF), VMEM((2, 8, 16, 128), BF),
+            VMEM((20, 8, 128), F32), VMEM((16, 8, 128), F32),
+            VMEM((3, 5, 8, 128), F32), VMEM((3, 4, 8, 128), F32),
+            VMEM((3, 5, 8, 128), BF), VMEM((3, 4, 8, 128), BF),
+            VMEM((3, 5, 8, 128), BF), VMEM((3, 4, 8, 128), BF),
+            VMEM((5, 8, 128), BF), VMEM((4, 8, 128), BF),
+            VMEM((2, 20, 8, 128), BF), VMEM((2, 16, 8, 128), BF),
             VMEM((2, 192, 256), F32), VMEM((192, 256), F32), VMEM((192, 512), F32),
             VMEM((2, 2, 64, 384), BF), VMEM((2, 64, 384), BF),
             dma, dma,

time: 52.9 us -> 51.9 us (0.981)
  Pallas kernels: 52.2 us -> 51.2 us
    pallas_call x1, Pallas kernels: 50.6 us -> 49.6 us  [shards(): pl.pallas_call(lambda *refs: kernel(n_norm, *refs), out_shape=(jax.ShapeD...]
where the time goes in v7:
time: 51.9 us; the launch traced here: 51.8 us
  Pallas kernels  51.2 us (99%)
  between operations  0.64 us (1%)
    pallas_call x1, Pallas kernels, shards(): pl.pallas_call(lambda *refs: kernel(n_norm, *refs), out_shape=(jax.ShapeD...  49.6 us
    pallas_call x1, Pallas kernels, shards(): pl.pallas_call(finish, out_shape=(jax.ShapeDtypeStruct((2, 64, 384), BF),...  1.54 us

profile of v7, /device:TPU:2, one launch (start us, length us, event | category | flops | bytes accessed | tf_op | source)
XLA Modules:
  0.0 51.8 jit_solution(4139396207933613832)
XLA Ops:
  0.6 49.6 %backward.1 = (bf16[2,64,384]{2,1,0:T(8,128)(2,1)S(1)}, bf16[2,36,8,128]{3,2,1,0:T(8,128)(2,1)S(1)}) custom-call(bf16[2,64,384]{2,1,0:T(8,128)(2,1)} %bitcast.6, bf16[2,2,192,128]{3,2,1,0:T(8,128)(2,1)} %bitcast.5, bf16[12,27,192]{2,1,0:T(8,128)(2,1)} %refs_2_.1, f32[384]{0:T(512)} %refs_3_.1, f32[384]{0:T(512)} %refs_4_.1), custom_call_target="tpu_custom_call" | custom-call | tf_op jit(solution)/shard_map/backward/pallas_call | solution.py:493
  50.3 1.5 %finish.1 = (bf16[2,64,384]{2,1,0:T(8,128)(2,1)}, f32[12,27,192]{2,1,0:T(8,128)}) custom-call(bf16[2,64,384]{2,1,0:T(8,128)(2,1)S(1)} %get-tuple-element.6.dacts_in, bf16[2,36,8,128]{3,2,1,0:T(8,128)(2,1)S(1)} %get-tuple-element.7.zout), custom_call_target="tpu_custom_call" | custom-call | tf_op jit(solution)/shard_map/finish/pallas_call | solution.py:522

commit v8 on v7

--- a/solution.py
+++ b/solution.py
@@ -16,7 +16,7 @@
 LANES = (1408, 1280)
 CUTS = (768, 640)
 SEGMENTS = (((0, 0, 896, 0), (1, 0, 512, 896)), ((1, 512, 384, 0), (2, 0, 896, 384)))
-NARROW = (1, 2)
+NARROW = (1, 2, 3)
 STREAMS = ((0, 0, 768, 384), (1, 0, 640, 384), (0, 768, 640, 384), (1, 640, 640, 384))
 STREAM_SEGMENTS = (((0, 0, 768, 0),), ((1, 512, 384, 0), (2, 0, 256, 384)),
                    ((0, 768, 128, 0), (1, 0, 512, 128)), ((2, 256, 640, 0),))

time: 51.9 us -> 51.6 us (level)
  Pallas kernels: 51.2 us -> 50.6 us
    pallas_call x1, Pallas kernels: 49.6 us -> 49 us  [shards(): pl.pallas_call(lambda *refs: kernel(n_norm, *refs), out_shape=(jax.ShapeD...]
where the time goes in v8:
time: 51.6 us; the launch traced here: 51.2 us
  Pallas kernels  50.6 us (98%)
  between operations  0.64 us (1%)
    pallas_call x1, Pallas kernels, shards(): pl.pallas_call(lambda *refs: kernel(n_norm, *refs), out_shape=(jax.ShapeD...  49 us
    pallas_call x1, Pallas kernels, shards(): pl.pallas_call(finish, out_shape=(jax.ShapeDtypeStruct((2, 64, 384), BF),...  1.54 us

profile of v8, /device:TPU:2, one launch (start us, length us, event | category | flops | bytes accessed | tf_op | source)
XLA Modules:
  0.0 51.2 jit_solution(4069562222847527244)
XLA Ops:
  0.6 49.0 %backward.1 = (bf16[2,64,384]{2,1,0:T(8,128)(2,1)S(1)}, bf16[2,36,8,128]{3,2,1,0:T(8,128)(2,1)S(1)}) custom-call(bf16[2,64,384]{2,1,0:T(8,128)(2,1)} %bitcast.6, bf16[2,2,192,128]{3,2,1,0:T(8,128)(2,1)} %bitcast.5, bf16[12,27,192]{2,1,0:T(8,128)(2,1)} %refs_2_.1, f32[384]{0:T(512)} %refs_3_.1, f32[384]{0:T(512)} %refs_4_.1), custom_call_target="tpu_custom_call" | custom-call | tf_op jit(solution)/shard_map/backward/pallas_call | solution.py:493
  49.7 1.5 %finish.1 = (bf16[2,64,384]{2,1,0:T(8,128)(2,1)}, f32[12,27,192]{2,1,0:T(8,128)}) custom-call(bf16[2,64,384]{2,1,0:T(8,128)(2,1)S(1)} %get-tuple-element.6.dacts_in, bf16[2,36,8,128]{3,2,1,0:T(8,128)(2,1)S(1)} %get-tuple-element.7.zout), custom_call_target="tpu_custom_call" | custom-call | tf_op jit(solution)/shard_map/finish/pallas_call | solution.py:522
